TPU v7x, 32 devices: a whole 2x2x4 slice. The times are simulated.
32 devices in a mesh: clips: 2 (over x), tile: 4 (over y, core), tm: 4 (over z).
Axes of the slice: x: 2, y: 2, z: 4, core: 2. Of those that a mesh axis runs over, the one named last changes fastest.
Arguments:
- clip_frames: bfloat16 [16, 16, 128, 256], P(('clips', 'tm'), 'tile'), parts along dimension 0, may hold values from -6 to 6
- weight_first: bfloat16 [3, 3, 3, 256, 256], replicated, may hold values from -0.078125 to 0.078125
- bias_first: float32 [256], replicated, may hold values from -3 to 3
- weight_second: bfloat16 [3, 3, 3, 256, 256], replicated, may hold values from -0.078125 to 0.078125
- bias_second: float32 [256], replicated, may hold values from -3 to 3
Outputs:
- pooled_frames: bfloat16 [8, 16, 128, 256], P(('clips', 'tm'), 'tile'), parts along dimension 0
There are 2 independent parts, one for each index of `clips`. A program takes and returns all parts, laid end to end along the dimension named above; an argument that names none is the same for every part. Nothing has to cross between parts.
All inputs are finite; a program needn't handle non-finite values.
Results may differ from a plain program's by a relative error of at most 0.0029.
Values may be sent and summed in bfloat16 or wider, within the bound.
No kernel may reach another device: no remote copies, remote signals or barrier semaphores. Data moves between devices by JAX's collectives and lax.ppermute only.
A program may use at most 128 MiB of HBM per device.

v0:
```python
import functools

import jax
import jax.numpy as jnp
from jax import lax
from jax.experimental import pallas as pl
from jax.experimental.pallas import tpu as pltpu
from jax.sharding import PartitionSpec as P


VMEM = pl.BlockSpec(memory_space=pltpu.VMEM)
HBM = pl.BlockSpec(memory_space=pltpu.HBM)


def call(body, outs, args, flops, in_specs=None, scratch=()):
    return pl.pallas_call(
        body,
        out_shape=outs,
        in_specs=in_specs or [VMEM] * len(args),
        out_specs=[VMEM] * len(outs),
        scratch_shapes=scratch,
        compiler_params=pltpu.CompilerParams(vmem_limit_bytes=16 << 20),
        cost_estimate=pl.CostEstimate(flops=flops, bytes_accessed=0, transcendentals=0),
    )(*args)


def flat(value):
    return value.reshape(-1, value.shape[-1])


def row_taps(slab, rows):
    return [flat(slab[p : p + rows]) for p in range(3)]


def convolved(lhs, weights, rows, cols):
    stacked = jnp.concatenate(lhs, axis=1)
    total = None
    for q in range(3):
        taps = jnp.concatenate([w[q] for w in weights], axis=0)
        part = jnp.dot(stacked, taps, preferred_element_type=jnp.float32)
        part = part.reshape(rows, cols, part.shape[-1])
        if q != 1:
            col = lax.broadcasted_iota(jnp.int32, part.shape, 1)
            edge = 0 if q == 0 else cols - 1
            part = jnp.where(col == edge, 0.0, pltpu.roll(part, 1 if q == 0 else cols - 1, 1))
        total = part if total is None else total + part
    return total


def parity():
    return lax.rem(lax.axis_index("tile"), 2)


def slab_of(outer, outer_half, inner_half, inner):
    even = parity() == 0
    blocks = [(outer, inner), (outer_half, inner_half), (inner_half, outer_half), (inner, outer)]
    return jnp.concatenate([jnp.where(even, a, b) for a, b in blocks], axis=0)


def own_slab(x, outer, inner):
    even = parity() == 0
    up, down = jnp.where(even, outer, inner), jnp.where(even, inner, outer)
    return jnp.concatenate([up, x, down], axis=0)


def weight_rows(w_ref, a):
    return [[w_ref[a, p, q] for q in range(3)] for p in range(3)]


def silu_rows(value, tiles):
    tile = lax.axis_index("tile")
    hidden = (value / (1.0 + jnp.exp(-value))).astype(jnp.bfloat16)
    row = lax.broadcasted_iota(jnp.int32, hidden.shape, 0)
    outside = ((row == 0) & (tile == 0)) | ((row == hidden.shape[0] - 1) & (tile == tiles - 1))
    return jnp.where(outside, jnp.zeros_like(hidden), hidden)


def pick_body(x_ref, own_ref, first_ref, second_ref, outer_ref, inner_ref, sems):
    rows = x_ref.shape[1]
    half = rows // 2
    odd = parity()
    outer_half, inner_half = pl.ds(odd * half, half), pl.ds((1 - odd) * half, half)
    outer, inner = pl.ds(odd * (rows - 2), 2), pl.ds((1 - odd) * (rows - 2), 2)
    moves = [
        (x_ref.at[1, outer_half], first_ref.at[pl.ds(0, half)]),
        (x_ref.at[1, inner_half], first_ref.at[pl.ds(half, half)]),
        (x_ref.at[0, inner_half], first_ref.at[pl.ds(2 * half, half)]),
        (x_ref.at[0, outer_half], second_ref),
        (x_ref.at[:, outer], outer_ref),
        (x_ref.at[:, inner], inner_ref),
        (x_ref, own_ref),
    ]
    copies = [pltpu.make_async_copy(a, b, sems.at[i]) for i, (a, b) in enumerate(moves)]
    for copy in copies:
        copy.start()
    for copy in copies:
        copy.wait()


def own1_body(x_ref, outer_ref, inner_ref, w_ref, b_ref, acc_ref):
    rows, cols = acc_ref.shape[:2]
    taps = []
    for f in range(2):
        taps += row_taps(own_slab(x_ref[f], outer_ref[f], inner_ref[f]), rows)
    weights = weight_rows(w_ref, 1) + weight_rows(w_ref, 2)
    acc_ref[...] = b_ref[...] + convolved(taps, weights, rows, cols)


def own0_body(x_ref, outer_ref, inner_ref, w_ref, b_ref, acc_ref):
    rows, cols = acc_ref.shape[:2]
    taps = row_taps(own_slab(x_ref[0], outer_ref[0], inner_ref[0]), rows)
    acc_ref[...] = b_ref[...] + convolved(taps, weight_rows(w_ref, 2), rows, cols)


def late_body(
    tiles, first_ref, inner_ref, outer_ref, w_ref, v_ref, acc0_ref, acc1_ref,
    sum0_ref, part_ref, rest_ref,
):
    rows, cols = acc0_ref.shape[:2]
    half = (rows - 2) // 2
    slab = slab_of(outer_ref[1], first_ref[:half], first_ref[half : 2 * half], inner_ref[0])
    taps = row_taps(slab, rows)
    acc1 = acc1_ref[...] + convolved(taps, weight_rows(w_ref, 0), rows, cols)
    h1 = silu_rows(acc1, tiles)
    sum0_ref[...] = acc0_ref[...] + convolved(taps, weight_rows(w_ref, 1), rows, cols)
    taps = row_taps(h1, rows - 2)
    part_ref[...] = convolved(
        taps + taps, weight_rows(v_ref, 0) + weight_rows(v_ref, 1), rows - 2, cols
    )
    rest_ref[...] = convolved(taps, weight_rows(v_ref, 2), rows - 2, cols)


def early_body(
    tiles, first_ref, second_ref, inner_ref, outer_ref, w_ref, v_ref, sum0_ref, part_ref,
    send_ref, h0_ref,
):
    rows, cols = sum0_ref.shape[:2]
    half = (rows - 2) // 2
    slab = slab_of(outer_ref[0], second_ref[...], first_ref[2 * half :], inner_ref[1])
    acc0 = sum0_ref[...] + convolved(row_taps(slab, rows), weight_rows(w_ref, 0), rows, cols)
    h0 = silu_rows(acc0, tiles)
    h0_ref[...] = h0
    part = part_ref[...] + convolved(
        row_taps(h0, rows - 2), weight_rows(v_ref, 0), rows - 2, cols
    )
    send_ref[0] = part.astype(jnp.bfloat16)


def rest_body(x_ref, h0_ref, rest_ref, v_ref, b_ref, out_ref):
    rows, cols = x_ref.shape[1:3]
    taps = row_taps(h0_ref[...], rows)
    part = rest_ref[...] + convolved(
        taps + taps, weight_rows(v_ref, 1) + weight_rows(v_ref, 2), rows, cols
    )
    both = x_ref[0].astype(jnp.float32) + x_ref[1].astype(jnp.float32)
    out_ref[0] = (both + part) * 0.5 + b_ref[...]


def block(x, weight_first, bias_first, weight_second, bias_second):
    _, rows, cols, channels = x.shape
    half = rows // 2
    tiles, times = lax.axis_size("tile"), lax.axis_size("tm")
    forward = [(i, i + 1) for i in range(times - 1)]
    inner_pairs = [(i, i + 1) for i in range(0, tiles - 1, 2)]
    outer_pairs = [(i, i + 1) for i in range(1, tiles - 1, 2)]
    inner_pairs += [(j, i) for i, j in inner_pairs]
    outer_pairs += [(j, i) for i, j in outer_pairs]
    diagonal = [(i * times + s, j * times + t) for i, j in outer_pairs for s, t in forward]

    def frames(*lead, dtype=jnp.bfloat16):
        return jax.ShapeDtypeStruct((*lead, cols, channels), dtype)

    f32 = jnp.float32
    own, first, second, outer_edge, inner_edge = call(
        pick_body,
        [frames(2, rows), frames(3 * half), frames(half), frames(2, 2), frames(2, 2)],
        (x,),
        10**10,
        in_specs=[HBM],
        scratch=[pltpu.SemaphoreType.DMA((7,))],
    )
    first = lax.ppermute(first, "tm", forward)
    outer = lax.ppermute(outer_edge, "tile", outer_pairs)
    inner = lax.ppermute(inner_edge, "tile", inner_pairs)
    corner = lax.ppermute(outer_edge, ("tile", "tm"), diagonal)
    second = lax.ppermute(second, "tm", forward)

    bias_first = bias_first.reshape(1, 1, -1)
    bias_second = bias_second.reshape(1, 1, -1)
    unit = 2 * 9 * channels * channels * cols
    wide = rows + 2
    (acc1,) = call(
        own1_body,
        [frames(wide, dtype=f32)],
        (own, outer, inner, weight_first, bias_first),
        2 * unit * wide,
    )
    (acc0,) = call(
        own0_body,
        [frames(wide, dtype=f32)],
        (own, outer, inner, weight_first, bias_first),
        unit * wide,
    )
    even = lax.rem(lax.axis_index("tile"), 2) == 0
    late_half, early_half = first[half : 2 * half], first[2 * half :]
    halves = jnp.stack([late_half, early_half])
    inner_corner = lax.ppermute(
        jnp.where(even, halves[:, half - 2 :], halves[:, :2]), "tile", inner_pairs
    )
    sum0, part, rest = call(
        functools.partial(late_body, tiles),
        [frames(wide, dtype=f32), frames(rows, dtype=f32), frames(rows, dtype=f32)],
        (first, inner_corner, corner, weight_first, weight_second, acc0, acc1),
        unit * (2 * wide + 3 * rows),
    )
    send, h0 = call(
        functools.partial(early_body, tiles),
        [frames(1, rows), frames(wide)],
        (first, second, inner_corner, corner, weight_first, weight_second, sum0, part),
        unit * (rows + wide),
    )
    before = lax.ppermute(send, "tm", forward)
    (rest,) = call(
        rest_body,
        [frames(1, rows, dtype=f32)],
        (own, h0, rest, weight_second, bias_second),
        2 * unit * rows,
    )
    return (rest + 0.5 * before.astype(f32)).astype(jnp.bfloat16)


def solution(mesh):
    in_specs = (P(("clips", "tm"), "tile", None, None), P(), P(), P(), P())
    out_specs = P(("clips", "tm"), "tile", None, None)
    return jax.shard_map(block, mesh=mesh, in_specs=in_specs, out_specs=out_specs, check_vma=False)
```

profile of v0, /device:TPU:0, one launch (start us, length us, event | category | flops | bytes accessed | tf_op | source)
XLA Modules:
  0.0 40.4 jit_solution(6459061087217092357)
XLA Ops:
  0.0 0.0 copy-start
  0.0 0.0 copy-start.2
  0.0 0.0 copy-start.4
  0.0 1.2 %copy-done.4 = bf16[2,4,128,256]{3,2,1,0:T(8,128)(2,1)S(1)} copy-done((bf16[2,4,128,256]{3,2,1,0:T(8,128)(2,1)S(1)}, bf16[2,4,128,256]{3,2,1,0:T(8,128)(2,1)}, u32[]{:S(2)}) %copy-start.4) | copy-done | bytes 524312
  1.2 0.8 %shard_map.55 = (bf16[2,4,128,256]{3,2,1,0:T(8,128)(2,1)S(1)}, bf16[6,128,256]{2,1,0:T(8,128)(2,1)S(1)}, bf16[2,128,256]{2,1,0:T(8,128)(2,1)S(1)}, bf16[2,2,128,...) custom-call(bf16[2,4,128,256]{3,2,1,0:T(8,128)(2,1)S(1)} %copy-done.4), custom_call_target="tpu_custom_call" | custom-call | flops 10000000000 | tf_op jit(solution)/shard_map/pallas_call | solution.py:16
  2.0 5.0 %collective-permute-start = (bf16[6,128,256]{2,1,0:T(8,128)(2,1)S(1)}, bf16[6,128,256]{2,1,0:T(8,128)(2,1)S(1)}, u32[]{:S(2)}, u32[]{:S(2)}) collective-permute-start(bf16[6,128,256]{2,1,0:T(8,128)(2,1)S(1)} %get-tuple-element.16), channel_id=1, source_target_pairs={{0,1},{1,2},{2,3},{4,5},{5,6},{6,7},{8,9},{9,10},{10,11},{12,13},{... | collective-permute-start | bytes 1179656 | tf_op jit(solution)/shard_map/ppermute | solution.py:182
  7.0 0.7 %collective-permute-start.4 = (bf16[2,2,128,256]{3,2,1,0:T(8,128)(2,1)S(1)}, bf16[2,2,128,256]{3,2,1,0:T(8,128)(2,1)S(1)}, u32[]{:S(2)}, u32[]{:S(2)}) collective-permute-start(bf16[2,2,128,256]{3,2,1,0:T(8,128)(2,1)S(1)} %get-tuple-element.18), channel_id=1, source_target_pairs={{4,8},{8,4},{5,9},{9,5},{6,10},{10,6},{7,11},{11,7},{20,24},{24,20... | collective-permute-start | bytes 786440 | tf_op jit(solution)/shard_map/ppermute | solution.py:183
  7.7 0.7 %collective-permute-start.3 = (bf16[2,2,128,256]{3,2,1,0:T(8,128)(2,1)S(1)}, bf16[2,2,128,256]{3,2,1,0:T(8,128)(2,1)S(1)}, u32[]{:S(2)}, u32[]{:S(2)}) collective-permute-start(bf16[2,2,128,256]{3,2,1,0:T(8,128)(2,1)S(1)} %get-tuple-element.18), channel_id=1, source_target_pairs={{4,9},{5,10},{6,11},{8,5},{9,6},{10,7},{20,25},{21,26},{22,27},{24... | collective-permute-start | bytes 786440 | tf_op jit(solution)/shard_map/ppermute | solution.py:185
  8.4 5.2 %collective-permute-start.5 = (bf16[2,2,128,256]{3,2,1,0:T(8,128)(2,1)S(1)}, bf16[2,2,128,256]{3,2,1,0:T(8,128)(2,1)S(1)}, u32[]{:S(2)}, u32[]{:S(2)}) collective-permute-start(bf16[2,2,128,256]{3,2,1,0:T(8,128)(2,1)S(1)} %get-tuple-element.19), channel_id=1, source_target_pairs={{0,4},{8,12},{4,0},{12,8},{1,5},{9,13},{5,1},{13,9},{2,6},{10,14},... | collective-permute-start | bytes 786440 | tf_op jit(solution)/shard_map/ppermute | solution.py:184
  13.5 2.9 %collective-permute-done.first_ref = bf16[6,128,256]{2,1,0:T(8,128)(2,1)S(1)} collective-permute-done((bf16[6,128,256]{2,1,0:T(8,128)(2,1)S(1)}, bf16[6,128,256]{2,1,0:T(8,128)(2,1)S(1)}, u32[]{:S(2)}, u32[]{:S(2)}) %collective-permute-start) | collective-permute-done | bytes 393248 | tf_op jit(solution)/shard_map/ppermute | solution.py:182
  16.5 0.1 collective-permute-start.2
  16.6 4.4 %collective-permute-start.1 = (bf16[2,128,256]{2,1,0:T(8,128)(2,1)S(1)}, bf16[2,128,256]{2,1,0:T(8,128)(2,1)S(1)}, u32[]{:S(2)}, u32[]{:S(2)}) collective-permute-start(bf16[2,128,256]{2,1,0:T(8,128)(2,1)S(1)} %get-tuple-element.17), channel_id=1, source_target_pairs={{0,1},{1,2},{2,3},{4,5},{5,6},{6,7},{8,9},{9,10},{10,11},{12,13},{... | collective-permute-start | bytes 393224 | tf_op jit(solution)/shard_map/ppermute | solution.py:186
  21.0 0.0 collective-permute-done.5.inner_ref
  21.0 0.0 collective-permute-done.4.outer_ref
  21.0 0.0 copy-done
  21.0 0.0 copy-done.2
  21.0 1.1 %shard_map.56.acc0_ref = f32[6,128,256]{2,1,0:T(8,128)S(1)} custom-call(bf16[2,4,128,256]{3,2,1,0:T(8,128)(2,1)S(1)} %get-tuple-element.15.x_ref, bf16[2,2,128,256]{3,2,1,0:T(8,128)(2,1)S(1)} %collective-permute-done.4.outer_ref, bf16[2,2,128,256]{3,2,1,0:T(8,128)(2,1)S(1)} %collective-permute-done.5.inner_ref, bf16[3,3,3,256,256]{4,3,2,1,0:T(8,128)(2,1)S(1)} %copy-done, ...), custom_call_target="tpu_custom_call" | custom-call | flops 905969664 | tf_op jit(solution)/shard_map/pallas_call | solution.py:16
  22.1 0.0 copy-start.1
  22.1 2.0 %shard_map.57.acc1_ref = f32[6,128,256]{2,1,0:T(8,128)S(1)} custom-call(bf16[2,4,128,256]{3,2,1,0:T(8,128)(2,1)S(1)} %get-tuple-element.15.x_ref, bf16[2,2,128,256]{3,2,1,0:T(8,128)(2,1)S(1)} %collective-permute-done.4.outer_ref, bf16[2,2,128,256]{3,2,1,0:T(8,128)(2,1)S(1)} %collective-permute-done.5.inner_ref, bf16[3,3,3,256,256]{4,3,2,1,0:T(8,128)(2,1)S(1)} %copy-done, ...), custom_call_target="tpu_custom_call" | custom-call | flops 1811939328 | tf_op jit(solution)/shard_map/pallas_call | solution.py:16
  24.1 0.0 collective-permute-done.3.outer_ref
  24.1 0.0 collective-permute-done.2.inner_ref
  24.2 0.0 copy-done.1
  24.2 3.9 %shard_map.58 = (f32[6,128,256]{2,1,0:T(8,128)S(1)}, f32[4,128,256]{2,1,0:T(8,128)S(1)}, f32[4,128,256]{2,1,0:T(8,128)S(1)}) custom-call(bf16[6,128,256]{2,1,0:T(8,128)(2,1)S(1)} %collective-permute-done.first_ref, bf16[2,2,128,256]{3,2,1,0:T(8,128)(2,1)S(1)} %collective-permute-done.2.inner_ref, ...), custom_call_target="tpu_custom_call" | custom-call | flops 3623878656 | tf_op jit(solution)/shard_map/pallas_call | solution.py:16
  28.0 0.0 collective-permute-done.1.second_ref
  28.1 0.0 copy-start.3
  28.1 2.1 %shard_map.59 = (bf16[1,4,128,256]{3,2,1,0:T(8,128)(2,1)S(1)}, bf16[6,128,256]{2,1,0:T(8,128)(2,1)S(1)}) custom-call(bf16[6,128,256]{2,1,0:T(8,128)(2,1)S(1)} %collective-permute-done.first_ref, bf16[2,128,256]{2,1,0:T(8,128)(2,1)S(1)} %collective-permute-done.1.second_ref, bf16[2,2,128,256]{3,2,1,0:T(8,128)(2,1)S(1)} %collective-permute-done.2.inner_ref, ...), custom_call_target="tpu_custom_call" | custom-call | flops 1509949440 | tf_op jit(solution)/shard_map/pallas_call | solution.py:16
  30.2 3.5 %collective-permute-start.6 = (bf16[1,4,128,256]{3,2,1,0:T(8,128)(2,1)S(1)}, bf16[1,4,128,256]{3,2,1,0:T(8,128)(2,1)S(1)}, u32[]{:S(2)}, u32[]{:S(2)}) collective-permute-start(bf16[1,4,128,256]{3,2,1,0:T(8,128)(2,1)S(1)} %get-tuple-element.24), channel_id=1, source_target_pairs={{0,1},{1,2},{2,3},{4,5},{5,6},{6,7},{8,9},{9,10},{10,11},{12,13},{... | collective-permute-start | bytes 786440 | tf_op jit(solution)/shard_map/ppermute | solution.py:222
  33.7 0.0 copy-done.3
  33.7 1.4 %shard_map.60 = f32[1,4,128,256]{3,2,1,0:T(8,128)S(1)} custom-call(bf16[2,4,128,256]{3,2,1,0:T(8,128)(2,1)S(1)} %get-tuple-element.15.x_ref, bf16[6,128,256]{2,1,0:T(8,128)(2,1)S(1)} %get-tuple-element.22.h0_ref, f32[4,128,256]{2,1,0:T(8,128)S(1)} %get-tuple-element.23.rest_ref, bf16[3,3,3,256,256]{4,3,2,1,0:T(8,128)(2,1)S(1)} %copy-done.1, ...), custom_call_target="tpu_custom_call" | custom-call | flops 1207959552 | tf_op jit(solution)/shard_map/pallas_call | solution.py:16
  35.1 4.5 %collective-permute-done.6 = bf16[1,4,128,256]{3,2,1,0:T(8,128)(2,1)S(1)} collective-permute-done((bf16[1,4,128,256]{3,2,1,0:T(8,128)(2,1)S(1)}, bf16[1,4,128,256]{3,2,1,0:T(8,128)(2,1)S(1)}, u32[]{:S(2)}, u32[]{:S(2)}) %collective-permute-start.6) | collective-permute-done | bytes 262176 | tf_op jit(solution)/shard_map/ppermute | solution.py:222
  39.6 0.8 %add_convert_fusion = bf16[1,4,128,256]{3,2,1,0:T(8,128)(2,1)} fusion(f32[1,4,128,256]{3,2,1,0:T(8,128)S(1)} %shard_map.60, bf16[1,4,128,256]{3,2,1,0:T(8,128)(2,1)S(1)} %collective-permute-done.6), kind=kLoop, calls=%fused_computation | loop fusion | flops 524288 | bytes 1048576 | tf_op jit(solution)/shard_map/convert_element_type | solution.py:229
  (2 shorter events, 0.0 us)
Async XLA Ops:
  0.0 21.0 %copy-start = (bf16[3,3,3,256,256]{4,3,2,1,0:T(8,128)(2,1)S(1)}, bf16[3,3,3,256,256]{4,3,2,1,0:T(8,128)(2,1)}, u32[]{:S(2)}) copy-start(bf16[3,3,3,256,256]{4,3,2,1,0:T(8,128)(2,1)} %w_ref.7) | copy-start | bytes 10616836
  0.0 21.0 %copy-start.2 = (f32[256]{0:T(256)S(1)}, f32[256]{0:T(256)}, u32[]{:S(2)}) copy-start(f32[256]{0:T(256)} %param.7) | copy-start | bytes 3076
  0.0 1.2 %copy-start.4 = (bf16[2,4,128,256]{3,2,1,0:T(8,128)(2,1)S(1)}, bf16[2,4,128,256]{3,2,1,0:T(8,128)(2,1)}, u32[]{:S(2)}) copy-start(bf16[2,4,128,256]{3,2,1,0:T(8,128)(2,1)} %x_ref.1) | copy-start | bytes 1572868
  2.0 14.4 %collective-permute-start = (bf16[6,128,256]{2,1,0:T(8,128)(2,1)S(1)}, bf16[6,128,256]{2,1,0:T(8,128)(2,1)S(1)}, u32[]{:S(2)}, u32[]{:S(2)}) collective-permute-start(bf16[6,128,256]{2,1,0:T(8,128)(2,1)S(1)} %get-tuple-element.16), channel_id=1, source_target_pairs={{0,1},{1,2},{2,3},{4,5},{5,6},{6,7},{8,9},{9,10},{10,11},{12,13},{... | collective-permute-start | bytes 1179656 | tf_op jit(solution)/shard_map/ppermute | solution.py:182
  7.0 14.0 %collective-permute-start.4 = (bf16[2,2,128,256]{3,2,1,0:T(8,128)(2,1)S(1)}, bf16[2,2,128,256]{3,2,1,0:T(8,128)(2,1)S(1)}, u32[]{:S(2)}, u32[]{:S(2)}) collective-permute-start(bf16[2,2,128,256]{3,2,1,0:T(8,128)(2,1)S(1)} %get-tuple-element.18), channel_id=1, source_target_pairs={{4,8},{8,4},{5,9},{9,5},{6,10},{10,6},{7,11},{11,7},{20,24},{24,20... | collective-permute-start | bytes 786440 | tf_op jit(solution)/shard_map/ppermute | solution.py:183
  7.7 16.5 %collective-permute-start.3 = (bf16[2,2,128,256]{3,2,1,0:T(8,128)(2,1)S(1)}, bf16[2,2,128,256]{3,2,1,0:T(8,128)(2,1)S(1)}, u32[]{:S(2)}, u32[]{:S(2)}) collective-permute-start(bf16[2,2,128,256]{3,2,1,0:T(8,128)(2,1)S(1)} %get-tuple-element.18), channel_id=1, source_target_pairs={{4,9},{5,10},{6,11},{8,5},{9,6},{10,7},{20,25},{21,26},{22,27},{24... | collective-permute-start | bytes 786440 | tf_op jit(solution)/shard_map/ppermute | solution.py:185
  8.4 12.6 %collective-permute-start.5 = (bf16[2,2,128,256]{3,2,1,0:T(8,128)(2,1)S(1)}, bf16[2,2,128,256]{3,2,1,0:T(8,128)(2,1)S(1)}, u32[]{:S(2)}, u32[]{:S(2)}) collective-permute-start(bf16[2,2,128,256]{3,2,1,0:T(8,128)(2,1)S(1)} %get-tuple-element.19), channel_id=1, source_target_pairs={{0,4},{8,12},{4,0},{12,8},{1,5},{9,13},{5,1},{13,9},{2,6},{10,14},... | collective-permute-start | bytes 786440 | tf_op jit(solution)/shard_map/ppermute | solution.py:184
  16.5 7.6 %collective-permute-start.2 = (bf16[2,2,128,256]{3,2,1,0:T(8,128)(2,1)S(1)}, bf16[2,2,128,256]{3,2,1,0:T(8,128)(2,1)S(1)}, u32[]{:S(2)}, u32[]{:S(2)}) collective-permute-start(bf16[2,2,128,256]{3,2,1,0:T(8,128)(2,1)S(1)} %pad_maximum_fusion), channel_id=1, source_target_pairs={{0,4},{8,12},{4,0},{12,8},{1,5},{9,13},{5,1},{13,9},{2,6},{10,14},... | collective-permute-start | bytes 786440 | tf_op jit(solution)/shard_map/ppermute | solution.py:207
  16.6 11.5 %collective-permute-start.1 = (bf16[2,128,256]{2,1,0:T(8,128)(2,1)S(1)}, bf16[2,128,256]{2,1,0:T(8,128)(2,1)S(1)}, u32[]{:S(2)}, u32[]{:S(2)}) collective-permute-start(bf16[2,128,256]{2,1,0:T(8,128)(2,1)S(1)} %get-tuple-element.17), channel_id=1, source_target_pairs={{0,1},{1,2},{2,3},{4,5},{5,6},{6,7},{8,9},{9,10},{10,11},{12,13},{... | collective-permute-start | bytes 393224 | tf_op jit(solution)/shard_map/ppermute | solution.py:186
  22.1 2.0 %copy-start.1 = (bf16[3,3,3,256,256]{4,3,2,1,0:T(8,128)(2,1)S(1)}, bf16[3,3,3,256,256]{4,3,2,1,0:T(8,128)(2,1)}, u32[]{:S(2)}) copy-start(bf16[3,3,3,256,256]{4,3,2,1,0:T(8,128)(2,1)} %v_ref.5) | copy-start | bytes 10616836
  28.1 5.6 %copy-start.3 = (f32[256]{0:T(256)S(1)}, f32[256]{0:T(256)}, u32[]{:S(2)}) copy-start(f32[256]{0:T(256)} %param.9) | copy-start | bytes 3076
  30.2 9.4 %collective-permute-start.6 = (bf16[1,4,128,256]{3,2,1,0:T(8,128)(2,1)S(1)}, bf16[1,4,128,256]{3,2,1,0:T(8,128)(2,1)S(1)}, u32[]{:S(2)}, u32[]{:S(2)}) collective-permute-start(bf16[1,4,128,256]{3,2,1,0:T(8,128)(2,1)S(1)} %get-tuple-element.24), channel_id=1, source_target_pairs={{0,1},{1,2},{2,3},{4,5},{5,6},{6,7},{8,9},{9,10},{10,11},{12,13},{... | collective-permute-start | bytes 786440 | tf_op jit(solution)/shard_map/ppermute | solution.py:222
where the time goes:
time: 40.6 us; the launch traced here: 40.4 us
  starting transfers between devices  19.5 us (48%)
  Pallas kernels  11.3 us (28%)
  waiting for transfers between devices  7.39 us (18%)
  local copies, waits for them, and re-layouts  1.23 us (3%)
  other arithmetic  0.81 us (2%)
    pallas_call x6, Pallas kernels, call(): pl.pallas_call(body, out_shape=outs, in_specs=in_specs or [VMEM] * len(ar...  11.3 us
    ppermute x1, starting transfers between devices, block(): inner = lax.ppermute(inner_edge, 'tile', inner_pairs)  5.18 us
    ppermute x1, starting transfers between devices, block(): first = lax.ppermute(first, 'tm', forward)  4.98 us
    ppermute x1, waiting for transfers between devices, block(): before = lax.ppermute(send, 'tm', forward)  4.46 us
    ppermute x1, starting transfers between devices, block(): second = lax.ppermute(second, 'tm', forward)  4.39 us
    ppermute x1, starting transfers between devices, block(): before = lax.ppermute(send, 'tm', forward)  3.49 us
    ppermute x1, waiting for transfers between devices, block(): first = lax.ppermute(first, 'tm', forward)  2.91 us
    unnamed x10, local copies, waits for them, and re-layouts  1.21 us
  transfers between devices with their start and end apart: 7, of which 2 were waited for; matrix products, arithmetic and copies ran while one was open for 0% of the time, Pallas kernels for 21%

commit v1 on v0

--- a/solution.py
+++ b/solution.py
@@ -114,7 +114,7 @@
 
 def late_body(
     tiles, first_ref, inner_ref, outer_ref, w_ref, v_ref, acc0_ref, acc1_ref,
-    sum0_ref, part_ref, rest_ref,
+    sum0_ref, part_ref, h1_ref,
 ):
     rows, cols = acc0_ref.shape[:2]
     half = (rows - 2) // 2
@@ -122,12 +122,12 @@
     taps = row_taps(slab, rows)
     acc1 = acc1_ref[...] + convolved(taps, weight_rows(w_ref, 0), rows, cols)
     h1 = silu_rows(acc1, tiles)
+    h1_ref[...] = h1
     sum0_ref[...] = acc0_ref[...] + convolved(taps, weight_rows(w_ref, 1), rows, cols)
     taps = row_taps(h1, rows - 2)
     part_ref[...] = convolved(
         taps + taps, weight_rows(v_ref, 0) + weight_rows(v_ref, 1), rows - 2, cols
     )
-    rest_ref[...] = convolved(taps, weight_rows(v_ref, 2), rows - 2, cols)
 
 
 def early_body(
@@ -146,12 +146,11 @@
     send_ref[0] = part.astype(jnp.bfloat16)
 
 
-def rest_body(x_ref, h0_ref, rest_ref, v_ref, b_ref, out_ref):
+def rest_body(x_ref, h0_ref, h1_ref, v_ref, b_ref, out_ref):
     rows, cols = x_ref.shape[1:3]
     taps = row_taps(h0_ref[...], rows)
-    part = rest_ref[...] + convolved(
-        taps + taps, weight_rows(v_ref, 1) + weight_rows(v_ref, 2), rows, cols
-    )
+    weights = weight_rows(v_ref, 1) + 2 * weight_rows(v_ref, 2)
+    part = convolved(taps + taps + row_taps(h1_ref[...], rows), weights, rows, cols)
     both = x_ref[0].astype(jnp.float32) + x_ref[1].astype(jnp.float32)
     out_ref[0] = (both + part) * 0.5 + b_ref[...]
 
@@ -174,7 +173,7 @@
     own, first, second, outer_edge, inner_edge = call(
         pick_body,
         [frames(2, rows), frames(3 * half), frames(half), frames(2, 2), frames(2, 2)],
-        (x,),
+        (pltpu.with_memory_space_constraint(x, pltpu.HBM),),
         10**10,
         in_specs=[HBM],
         scratch=[pltpu.SemaphoreType.DMA((7,))],
@@ -207,11 +206,11 @@
     inner_corner = lax.ppermute(
         jnp.where(even, halves[:, half - 2 :], halves[:, :2]), "tile", inner_pairs
     )
-    sum0, part, rest = call(
+    sum0, part, h1 = call(
         functools.partial(late_body, tiles),
-        [frames(wide, dtype=f32), frames(rows, dtype=f32), frames(rows, dtype=f32)],
+        [frames(wide, dtype=f32), frames(rows, dtype=f32), frames(wide)],
         (first, inner_corner, corner, weight_first, weight_second, acc0, acc1),
-        unit * (2 * wide + 3 * rows),
+        unit * 2 * (wide + rows),
     )
     send, h0 = call(
         functools.partial(early_body, tiles),
@@ -223,8 +222,8 @@
     (rest,) = call(
         rest_body,
         [frames(1, rows, dtype=f32)],
-        (own, h0, rest, weight_second, bias_second),
-        2 * unit * rows,
+        (own, h0, h1, weight_second, bias_second),
+        3 * unit * rows,
     )
     return (rest + 0.5 * before.astype(f32)).astype(jnp.bfloat16)
 

time: 40.6 us -> 39.6 us (0.975)
  local copies, waits for them, and re-layouts: 1.23 us -> 0.04 us
  Pallas kernels: 11.3 us -> 12.1 us
  waiting for transfers between devices: 7.39 us -> 6.79 us
    unnamed x10 -> x8, local copies, waits for them, and re-layouts: 1.21 us -> 0.02 us
    pallas_call x6, Pallas kernels: 11.3 us -> 12.1 us  [call(): pl.pallas_call(body, out_shape=outs, in_specs=in_specs or [VMEM] * len(ar...]
    ppermute x1, waiting for transfers between devices: 4.46 us -> 3.87 us  [block(): before = lax.ppermute(send, 'tm', forward)]
where the time goes in v1:
time: 39.6 us; the launch traced here: 39.4 us
  starting transfers between devices  19.5 us (49%)
  Pallas kernels  12.1 us (31%)
  waiting for transfers between devices  6.79 us (17%)
  other arithmetic  0.79 us (2%)
    pallas_call x6, Pallas kernels, call(): pl.pallas_call(body, out_shape=outs, in_specs=in_specs or [VMEM] * len(ar...  12.1 us
    ppermute x1, starting transfers between devices, block(): inner = lax.ppermute(inner_edge, 'tile', inner_pairs)  5.18 us
    ppermute x1, starting transfers between devices, block(): first = lax.ppermute(first, 'tm', forward)  4.98 us
    ppermute x1, starting transfers between devices, block(): second = lax.ppermute(second, 'tm', forward)  4.39 us
    ppermute x1, waiting for transfers between devices, block(): before = lax.ppermute(send, 'tm', forward)  3.87 us
    ppermute x1, starting transfers between devices, block(): before = lax.ppermute(send, 'tm', forward)  3.5 us
    ppermute x1, waiting for transfers between devices, block(): first = lax.ppermute(first, 'tm', forward)  2.91 us
  transfers between devices with their start and end apart: 7, of which 2 were waited for; matrix products, arithmetic and copies ran while one was open for 0% of the time, Pallas kernels for 21%

profile of v1, /device:TPU:0, one launch (start us, length us, event | category | flops | bytes accessed | tf_op | source)
XLA Modules:
  0.0 39.4 jit_solution(3733828189560984095)
XLA Ops:
  0.0 0.0 copy-start
  0.0 0.0 copy-start.2
  0.0 1.7 %shard_map.55 = (bf16[2,4,128,256]{3,2,1,0:T(8,128)(2,1)S(1)}, bf16[6,128,256]{2,1,0:T(8,128)(2,1)S(1)}, bf16[2,128,256]{2,1,0:T(8,128)(2,1)S(1)}, bf16[2,2,128,...) custom-call(bf16[2,4,128,256]{3,2,1,0:T(8,128)(2,1)} %x_ref.1), custom_call_target="tpu_custom_call" | custom-call | flops 10000000000 | tf_op jit(solution)/shard_map/pallas_call | solution.py:16
  1.7 5.0 %collective-permute-start = (bf16[6,128,256]{2,1,0:T(8,128)(2,1)S(1)}, bf16[6,128,256]{2,1,0:T(8,128)(2,1)S(1)}, u32[]{:S(2)}, u32[]{:S(2)}) collective-permute-start(bf16[6,128,256]{2,1,0:T(8,128)(2,1)S(1)} %get-tuple-element.16), channel_id=1, source_target_pairs={{0,1},{1,2},{2,3},{4,5},{5,6},{6,7},{8,9},{9,10},{10,11},{12,13},{... | collective-permute-start | bytes 1179656 | tf_op jit(solution)/shard_map/ppermute | solution.py:181
  6.7 0.7 %collective-permute-start.4 = (bf16[2,2,128,256]{3,2,1,0:T(8,128)(2,1)S(1)}, bf16[2,2,128,256]{3,2,1,0:T(8,128)(2,1)S(1)}, u32[]{:S(2)}, u32[]{:S(2)}) collective-permute-start(bf16[2,2,128,256]{3,2,1,0:T(8,128)(2,1)S(1)} %get-tuple-element.18), channel_id=1, source_target_pairs={{4,8},{8,4},{5,9},{9,5},{6,10},{10,6},{7,11},{11,7},{20,24},{24,20... | collective-permute-start | bytes 786440 | tf_op jit(solution)/shard_map/ppermute | solution.py:182
  7.3 0.7 %collective-permute-start.3 = (bf16[2,2,128,256]{3,2,1,0:T(8,128)(2,1)S(1)}, bf16[2,2,128,256]{3,2,1,0:T(8,128)(2,1)S(1)}, u32[]{:S(2)}, u32[]{:S(2)}) collective-permute-start(bf16[2,2,128,256]{3,2,1,0:T(8,128)(2,1)S(1)} %get-tuple-element.18), channel_id=1, source_target_pairs={{4,9},{5,10},{6,11},{8,5},{9,6},{10,7},{20,25},{21,26},{22,27},{24... | collective-permute-start | bytes 786440 | tf_op jit(solution)/shard_map/ppermute | solution.py:184
  8.0 5.2 %collective-permute-start.5 = (bf16[2,2,128,256]{3,2,1,0:T(8,128)(2,1)S(1)}, bf16[2,2,128,256]{3,2,1,0:T(8,128)(2,1)S(1)}, u32[]{:S(2)}, u32[]{:S(2)}) collective-permute-start(bf16[2,2,128,256]{3,2,1,0:T(8,128)(2,1)S(1)} %get-tuple-element.19), channel_id=1, source_target_pairs={{0,4},{8,12},{4,0},{12,8},{1,5},{9,13},{5,1},{13,9},{2,6},{10,14},... | collective-permute-start | bytes 786440 | tf_op jit(solution)/shard_map/ppermute | solution.py:183
  13.2 2.9 %collective-permute-done.first_ref = bf16[6,128,256]{2,1,0:T(8,128)(2,1)S(1)} collective-permute-done((bf16[6,128,256]{2,1,0:T(8,128)(2,1)S(1)}, bf16[6,128,256]{2,1,0:T(8,128)(2,1)S(1)}, u32[]{:S(2)}, u32[]{:S(2)}) %collective-permute-start) | collective-permute-done | bytes 393248 | tf_op jit(solution)/shard_map/ppermute | solution.py:181
  16.2 0.1 collective-permute-start.2
  16.3 4.4 %collective-permute-start.1 = (bf16[2,128,256]{2,1,0:T(8,128)(2,1)S(1)}, bf16[2,128,256]{2,1,0:T(8,128)(2,1)S(1)}, u32[]{:S(2)}, u32[]{:S(2)}) collective-permute-start(bf16[2,128,256]{2,1,0:T(8,128)(2,1)S(1)} %get-tuple-element.17), channel_id=1, source_target_pairs={{0,1},{1,2},{2,3},{4,5},{5,6},{6,7},{8,9},{9,10},{10,11},{12,13},{... | collective-permute-start | bytes 393224 | tf_op jit(solution)/shard_map/ppermute | solution.py:185
  20.7 0.0 collective-permute-done.5.inner_ref
  20.7 0.0 collective-permute-done.4.outer_ref
  20.7 0.0 copy-done
  20.7 0.0 copy-done.2
  20.7 1.1 %shard_map.56.acc0_ref = f32[6,128,256]{2,1,0:T(8,128)S(1)} custom-call(bf16[2,4,128,256]{3,2,1,0:T(8,128)(2,1)S(1)} %get-tuple-element.15.x_ref, bf16[2,2,128,256]{3,2,1,0:T(8,128)(2,1)S(1)} %collective-permute-done.4.outer_ref, bf16[2,2,128,256]{3,2,1,0:T(8,128)(2,1)S(1)} %collective-permute-done.5.inner_ref, bf16[3,3,3,256,256]{4,3,2,1,0:T(8,128)(2,1)S(1)} %copy-done, ...), custom_call_target="tpu_custom_call" | custom-call | flops 905969664 | tf_op jit(solution)/shard_map/pallas_call | solution.py:16
  21.8 0.0 copy-start.1
  21.8 2.0 %shard_map.57.acc1_ref = f32[6,128,256]{2,1,0:T(8,128)S(1)} custom-call(bf16[2,4,128,256]{3,2,1,0:T(8,128)(2,1)S(1)} %get-tuple-element.15.x_ref, bf16[2,2,128,256]{3,2,1,0:T(8,128)(2,1)S(1)} %collective-permute-done.4.outer_ref, bf16[2,2,128,256]{3,2,1,0:T(8,128)(2,1)S(1)} %collective-permute-done.5.inner_ref, bf16[3,3,3,256,256]{4,3,2,1,0:T(8,128)(2,1)S(1)} %copy-done, ...), custom_call_target="tpu_custom_call" | custom-call | flops 1811939328 | tf_op jit(solution)/shard_map/pallas_call | solution.py:16
  23.8 0.0 collective-permute-done.3.outer_ref
  23.8 0.0 collective-permute-done.2.inner_ref
  23.8 0.0 copy-done.1
  23.9 3.2 %shard_map.58 = (f32[6,128,256]{2,1,0:T(8,128)S(1)}, f32[4,128,256]{2,1,0:T(8,128)S(1)}, bf16[6,128,256]{2,1,0:T(8,128)(2,1)S(1)}) custom-call(bf16[6,128,256]{2,1,0:T(8,128)(2,1)S(1)} %collective-permute-done.first_ref, bf16[2,2,128,256]{3,2,1,0:T(8,128)(2,1)S(1)} %collective-permute-done.2.inner_ref, ...), custom_call_target="tpu_custom_call" | custom-call | flops 3019898880 | tf_op jit(solution)/shard_map/pallas_call | solution.py:16
  27.1 0.0 collective-permute-done.1.second_ref
  27.1 0.0 copy-start.3
  27.1 2.1 %shard_map.59 = (bf16[1,4,128,256]{3,2,1,0:T(8,128)(2,1)S(1)}, bf16[6,128,256]{2,1,0:T(8,128)(2,1)S(1)}) custom-call(bf16[6,128,256]{2,1,0:T(8,128)(2,1)S(1)} %collective-permute-done.first_ref, bf16[2,128,256]{2,1,0:T(8,128)(2,1)S(1)} %collective-permute-done.1.second_ref, bf16[2,2,128,256]{3,2,1,0:T(8,128)(2,1)S(1)} %collective-permute-done.2.inner_ref, ...), custom_call_target="tpu_custom_call" | custom-call | flops 1509949440 | tf_op jit(solution)/shard_map/pallas_call | solution.py:16
  29.2 3.5 %collective-permute-start.6 = (bf16[1,4,128,256]{3,2,1,0:T(8,128)(2,1)S(1)}, bf16[1,4,128,256]{3,2,1,0:T(8,128)(2,1)S(1)}, u32[]{:S(2)}, u32[]{:S(2)}) collective-permute-start(bf16[1,4,128,256]{3,2,1,0:T(8,128)(2,1)S(1)} %get-tuple-element.24), channel_id=1, source_target_pairs={{0,1},{1,2},{2,3},{4,5},{5,6},{6,7},{8,9},{9,10},{10,11},{12,13},{... | collective-permute-start | bytes 786440 | tf_op jit(solution)/shard_map/ppermute | solution.py:221
  32.8 0.0 copy-done.3
  32.8 2.0 %shard_map.60 = f32[1,4,128,256]{3,2,1,0:T(8,128)S(1)} custom-call(bf16[2,4,128,256]{3,2,1,0:T(8,128)(2,1)S(1)} %get-tuple-element.15.x_ref, bf16[6,128,256]{2,1,0:T(8,128)(2,1)S(1)} %get-tuple-element.22.h0_ref, bf16[6,128,256]{2,1,0:T(8,128)(2,1)S(1)} %get-tuple-element.23.h1_ref, bf16[3,3,3,256,256]{4,3,2,1,0:T(8,128)(2,1)S(1)} %copy-done.1, ...), custom_call_target="tpu_custom_call" | custom-call | flops 1811939328 | tf_op jit(solution)/shard_map/pallas_call | solution.py:16
  34.8 3.9 %collective-permute-done.6 = bf16[1,4,128,256]{3,2,1,0:T(8,128)(2,1)S(1)} collective-permute-done((bf16[1,4,128,256]{3,2,1,0:T(8,128)(2,1)S(1)}, bf16[1,4,128,256]{3,2,1,0:T(8,128)(2,1)S(1)}, u32[]{:S(2)}, u32[]{:S(2)}) %collective-permute-start.6) | collective-permute-done | bytes 262176 | tf_op jit(solution)/shard_map/ppermute | solution.py:221
  38.6 0.8 %add_convert_fusion = bf16[1,4,128,256]{3,2,1,0:T(8,128)(2,1)} fusion(f32[1,4,128,256]{3,2,1,0:T(8,128)S(1)} %shard_map.60, bf16[1,4,128,256]{3,2,1,0:T(8,128)(2,1)S(1)} %collective-permute-done.6), kind=kLoop, calls=%fused_computation | loop fusion | flops 524288 | bytes 1048576 | tf_op jit(solution)/shard_map/convert_element_type | solution.py:228
  (2 shorter events, 0.0 us)
Async XLA Ops:
  0.0 20.7 %copy-start = (bf16[3,3,3,256,256]{4,3,2,1,0:T(8,128)(2,1)S(1)}, bf16[3,3,3,256,256]{4,3,2,1,0:T(8,128)(2,1)}, u32[]{:S(2)}) copy-start(bf16[3,3,3,256,256]{4,3,2,1,0:T(8,128)(2,1)} %w_ref.7) | copy-start | bytes 10616836
  0.0 20.7 %copy-start.2 = (f32[256]{0:T(256)S(1)}, f32[256]{0:T(256)}, u32[]{:S(2)}) copy-start(f32[256]{0:T(256)} %param.7) | copy-start | bytes 3076
  1.7 14.4 %collective-permute-start = (bf16[6,128,256]{2,1,0:T(8,128)(2,1)S(1)}, bf16[6,128,256]{2,1,0:T(8,128)(2,1)S(1)}, u32[]{:S(2)}, u32[]{:S(2)}) collective-permute-start(bf16[6,128,256]{2,1,0:T(8,128)(2,1)S(1)} %get-tuple-element.16), channel_id=1, source_target_pairs={{0,1},{1,2},{2,3},{4,5},{5,6},{6,7},{8,9},{9,10},{10,11},{12,13},{... | collective-permute-start | bytes 1179656 | tf_op jit(solution)/shard_map/ppermute | solution.py:181
  6.7 14.0 %collective-permute-start.4 = (bf16[2,2,128,256]{3,2,1,0:T(8,128)(2,1)S(1)}, bf16[2,2,128,256]{3,2,1,0:T(8,128)(2,1)S(1)}, u32[]{:S(2)}, u32[]{:S(2)}) collective-permute-start(bf16[2,2,128,256]{3,2,1,0:T(8,128)(2,1)S(1)} %get-tuple-element.18), channel_id=1, source_target_pairs={{4,8},{8,4},{5,9},{9,5},{6,10},{10,6},{7,11},{11,7},{20,24},{24,20... | collective-permute-start | bytes 786440 | tf_op jit(solution)/shard_map/ppermute | solution.py:182
  7.3 16.5 %collective-permute-start.3 = (bf16[2,2,128,256]{3,2,1,0:T(8,128)(2,1)S(1)}, bf16[2,2,128,256]{3,2,1,0:T(8,128)(2,1)S(1)}, u32[]{:S(2)}, u32[]{:S(2)}) collective-permute-start(bf16[2,2,128,256]{3,2,1,0:T(8,128)(2,1)S(1)} %get-tuple-element.18), channel_id=1, source_target_pairs={{4,9},{5,10},{6,11},{8,5},{9,6},{10,7},{20,25},{21,26},{22,27},{24... | collective-permute-start | bytes 786440 | tf_op jit(solution)/shard_map/ppermute | solution.py:184
  8.0 12.6 %collective-permute-start.5 = (bf16[2,2,128,256]{3,2,1,0:T(8,128)(2,1)S(1)}, bf16[2,2,128,256]{3,2,1,0:T(8,128)(2,1)S(1)}, u32[]{:S(2)}, u32[]{:S(2)}) collective-permute-start(bf16[2,2,128,256]{3,2,1,0:T(8,128)(2,1)S(1)} %get-tuple-element.19), channel_id=1, source_target_pairs={{0,4},{8,12},{4,0},{12,8},{1,5},{9,13},{5,1},{13,9},{2,6},{10,14},... | collective-permute-start | bytes 786440 | tf_op jit(solution)/shard_map/ppermute | solution.py:183
  16.2 7.7 %collective-permute-start.2 = (bf16[2,2,128,256]{3,2,1,0:T(8,128)(2,1)S(1)}, bf16[2,2,128,256]{3,2,1,0:T(8,128)(2,1)S(1)}, u32[]{:S(2)}, u32[]{:S(2)}) collective-permute-start(bf16[2,2,128,256]{3,2,1,0:T(8,128)(2,1)S(1)} %pad_maximum_fusion), channel_id=1, source_target_pairs={{0,4},{8,12},{4,0},{12,8},{1,5},{9,13},{5,1},{13,9},{2,6},{10,14},... | collective-permute-start | bytes 786440 | tf_op jit(solution)/shard_map/ppermute | solution.py:206
  16.3 10.8 %collective-permute-start.1 = (bf16[2,128,256]{2,1,0:T(8,128)(2,1)S(1)}, bf16[2,128,256]{2,1,0:T(8,128)(2,1)S(1)}, u32[]{:S(2)}, u32[]{:S(2)}) collective-permute-start(bf16[2,128,256]{2,1,0:T(8,128)(2,1)S(1)} %get-tuple-element.17), channel_id=1, source_target_pairs={{0,1},{1,2},{2,3},{4,5},{5,6},{6,7},{8,9},{9,10},{10,11},{12,13},{... | collective-permute-start | bytes 393224 | tf_op jit(solution)/shard_map/ppermute | solution.py:185
  21.8 2.0 %copy-start.1 = (bf16[3,3,3,256,256]{4,3,2,1,0:T(8,128)(2,1)S(1)}, bf16[3,3,3,256,256]{4,3,2,1,0:T(8,128)(2,1)}, u32[]{:S(2)}) copy-start(bf16[3,3,3,256,256]{4,3,2,1,0:T(8,128)(2,1)} %v_ref.5) | copy-start | bytes 10616836
  27.1 5.6 %copy-start.3 = (f32[256]{0:T(256)S(1)}, f32[256]{0:T(256)}, u32[]{:S(2)}) copy-start(f32[256]{0:T(256)} %param.9) | copy-start | bytes 3076
  29.2 9.4 %collective-permute-start.6 = (bf16[1,4,128,256]{3,2,1,0:T(8,128)(2,1)S(1)}, bf16[1,4,128,256]{3,2,1,0:T(8,128)(2,1)S(1)}, u32[]{:S(2)}, u32[]{:S(2)}) collective-permute-start(bf16[1,4,128,256]{3,2,1,0:T(8,128)(2,1)S(1)} %get-tuple-element.24), channel_id=1, source_target_pairs={{0,1},{1,2},{2,3},{4,5},{5,6},{6,7},{8,9},{9,10},{10,11},{12,13},{... | collective-permute-start | bytes 786440 | tf_op jit(solution)/shard_map/ppermute | solution.py:221

commit v2 on v1

--- a/solution.py
+++ b/solution.py
@@ -51,16 +51,25 @@
     return lax.rem(lax.axis_index("tile"), 2)
 
 
-def slab_of(outer, outer_half, inner_half, inner):
+def bounded(up, main, down, tiles):
+    tile = lax.axis_index("tile")
+    up = jnp.where(tile == 0, jnp.zeros_like(up), up)
+    down = jnp.where(tile == tiles - 1, jnp.zeros_like(down), down)
+    return jnp.concatenate([up, *main, down], axis=0)
+
+
+def slab_of(outer, outer_half, inner_half, inner, tiles):
     even = parity() == 0
-    blocks = [(outer, inner), (outer_half, inner_half), (inner_half, outer_half), (inner, outer)]
-    return jnp.concatenate([jnp.where(even, a, b) for a, b in blocks], axis=0)
-
-
-def own_slab(x, outer, inner):
+    main = [jnp.where(even, outer_half, inner_half), jnp.where(even, inner_half, outer_half)]
+    up, down = jnp.where(even, outer, inner), jnp.where(even, inner, outer)
+    slab = bounded(up, main, down, tiles)
+    return jnp.where(lax.axis_index("tm") == 0, jnp.zeros_like(slab), slab)
+
+
+def own_slab(x, outer, inner, tiles):
     even = parity() == 0
     up, down = jnp.where(even, outer, inner), jnp.where(even, inner, outer)
-    return jnp.concatenate([up, x, down], axis=0)
+    return bounded(up, [x], down, tiles)
 
 
 def weight_rows(w_ref, a):
@@ -75,40 +84,55 @@
     return jnp.where(outside, jnp.zeros_like(hidden), hidden)
 
 
-def pick_body(x_ref, own_ref, first_ref, second_ref, outer_ref, inner_ref, sems):
-    rows = x_ref.shape[1]
-    half = rows // 2
-    odd = parity()
-    outer_half, inner_half = pl.ds(odd * half, half), pl.ds((1 - odd) * half, half)
-    outer, inner = pl.ds(odd * (rows - 2), 2), pl.ds((1 - odd) * (rows - 2), 2)
-    moves = [
-        (x_ref.at[1, outer_half], first_ref.at[pl.ds(0, half)]),
-        (x_ref.at[1, inner_half], first_ref.at[pl.ds(half, half)]),
-        (x_ref.at[0, inner_half], first_ref.at[pl.ds(2 * half, half)]),
-        (x_ref.at[0, outer_half], second_ref),
-        (x_ref.at[:, outer], outer_ref),
-        (x_ref.at[:, inner], inner_ref),
-        (x_ref, own_ref),
-    ]
-    copies = [pltpu.make_async_copy(a, b, sems.at[i]) for i, (a, b) in enumerate(moves)]
+def move(pairs, sems):
+    copies = [pltpu.make_async_copy(a, b, sems.at[i]) for i, (a, b) in enumerate(pairs)]
     for copy in copies:
         copy.start()
     for copy in copies:
         copy.wait()
 
 
-def own1_body(x_ref, outer_ref, inner_ref, w_ref, b_ref, acc_ref):
+def halves_of(rows):
+    half, odd = rows // 2, parity()
+    return pl.ds(odd * half, half), pl.ds((1 - odd) * half, half)
+
+
+def cut_body(x_ref, first_ref, sems):
+    half = x_ref.shape[1] // 2
+    outer, inner = halves_of(2 * half)
+    pairs = [
+        (x_ref.at[1, outer], first_ref.at[pl.ds(0, half)]),
+        (x_ref.at[1, inner], first_ref.at[pl.ds(half, half)]),
+        (x_ref.at[0, inner], first_ref.at[pl.ds(2 * half, half)]),
+    ]
+    move(pairs, sems)
+
+
+def pick_body(x_ref, own_ref, second_ref, outer_ref, inner_ref, sems):
+    rows = x_ref.shape[1]
+    odd = parity()
+    outer, inner = pl.ds(odd * (rows - 2), 2), pl.ds((1 - odd) * (rows - 2), 2)
+    pairs = [
+        (x_ref.at[:, outer], outer_ref),
+        (x_ref.at[:, inner], inner_ref),
+        (x_ref.at[0, halves_of(rows)[0]], second_ref),
+        (x_ref, own_ref),
+    ]
+    move(pairs, sems)
+
+
+def own1_body(tiles, x_ref, outer_ref, inner_ref, w_ref, b_ref, acc_ref):
     rows, cols = acc_ref.shape[:2]
     taps = []
     for f in range(2):
-        taps += row_taps(own_slab(x_ref[f], outer_ref[f], inner_ref[f]), rows)
+        taps += row_taps(own_slab(x_ref[f], outer_ref[f], inner_ref[f], tiles), rows)
     weights = weight_rows(w_ref, 1) + weight_rows(w_ref, 2)
     acc_ref[...] = b_ref[...] + convolved(taps, weights, rows, cols)
 
 
-def own0_body(x_ref, outer_ref, inner_ref, w_ref, b_ref, acc_ref):
+def own0_body(tiles, x_ref, outer_ref, inner_ref, w_ref, b_ref, acc_ref):
     rows, cols = acc_ref.shape[:2]
-    taps = row_taps(own_slab(x_ref[0], outer_ref[0], inner_ref[0]), rows)
+    taps = row_taps(own_slab(x_ref[0], outer_ref[0], inner_ref[0], tiles), rows)
     acc_ref[...] = b_ref[...] + convolved(taps, weight_rows(w_ref, 2), rows, cols)
 
 
@@ -118,7 +142,7 @@
 ):
     rows, cols = acc0_ref.shape[:2]
     half = (rows - 2) // 2
-    slab = slab_of(outer_ref[1], first_ref[:half], first_ref[half : 2 * half], inner_ref[0])
+    slab = slab_of(outer_ref[1], first_ref[:half], first_ref[half : 2 * half], inner_ref[0], tiles)
     taps = row_taps(slab, rows)
     acc1 = acc1_ref[...] + convolved(taps, weight_rows(w_ref, 0), rows, cols)
     h1 = silu_rows(acc1, tiles)
@@ -136,7 +160,7 @@
 ):
     rows, cols = sum0_ref.shape[:2]
     half = (rows - 2) // 2
-    slab = slab_of(outer_ref[0], second_ref[...], first_ref[2 * half :], inner_ref[1])
+    slab = slab_of(outer_ref[0], second_ref[...], first_ref[2 * half :], inner_ref[1], tiles)
     acc0 = sum0_ref[...] + convolved(row_taps(slab, rows), weight_rows(w_ref, 0), rows, cols)
     h0 = silu_rows(acc0, tiles)
     h0_ref[...] = h0
@@ -160,42 +184,53 @@
     half = rows // 2
     tiles, times = lax.axis_size("tile"), lax.axis_size("tm")
     forward = [(i, i + 1) for i in range(times - 1)]
+    ring = forward + [(times - 1, 0)]
     inner_pairs = [(i, i + 1) for i in range(0, tiles - 1, 2)]
     outer_pairs = [(i, i + 1) for i in range(1, tiles - 1, 2)]
     inner_pairs += [(j, i) for i, j in inner_pairs]
     outer_pairs += [(j, i) for i, j in outer_pairs]
+    unpaired = [(0, tiles - 1), (tiles - 1, 0)] if tiles % 2 == 0 else []
     diagonal = [(i * times + s, j * times + t) for i, j in outer_pairs for s, t in forward]
 
     def frames(*lead, dtype=jnp.bfloat16):
         return jax.ShapeDtypeStruct((*lead, cols, channels), dtype)
 
     f32 = jnp.float32
-    own, first, second, outer_edge, inner_edge = call(
+    x_hbm = pltpu.with_memory_space_constraint(x, pltpu.HBM)
+    (first,) = call(
+        cut_body,
+        [frames(3 * half)],
+        (x_hbm,),
+        0,
+        in_specs=[HBM],
+        scratch=[pltpu.SemaphoreType.DMA((3,))],
+    )
+    own, second, outer_edge, inner_edge = call(
         pick_body,
-        [frames(2, rows), frames(3 * half), frames(half), frames(2, 2), frames(2, 2)],
-        (pltpu.with_memory_space_constraint(x, pltpu.HBM),),
+        [frames(2, rows), frames(half), frames(2, 2), frames(2, 2)],
+        (x_hbm,),
         10**10,
         in_specs=[HBM],
-        scratch=[pltpu.SemaphoreType.DMA((7,))],
-    )
-    first = lax.ppermute(first, "tm", forward)
-    outer = lax.ppermute(outer_edge, "tile", outer_pairs)
+        scratch=[pltpu.SemaphoreType.DMA((4,))],
+    )
+    first = lax.ppermute(first, "tm", ring)
+    outer = lax.ppermute(outer_edge, "tile", outer_pairs + unpaired)
     inner = lax.ppermute(inner_edge, "tile", inner_pairs)
     corner = lax.ppermute(outer_edge, ("tile", "tm"), diagonal)
-    second = lax.ppermute(second, "tm", forward)
+    second = lax.ppermute(second, "tm", ring)
 
     bias_first = bias_first.reshape(1, 1, -1)
     bias_second = bias_second.reshape(1, 1, -1)
     unit = 2 * 9 * channels * channels * cols
     wide = rows + 2
     (acc1,) = call(
-        own1_body,
+        functools.partial(own1_body, tiles),
         [frames(wide, dtype=f32)],
         (own, outer, inner, weight_first, bias_first),
         2 * unit * wide,
     )
     (acc0,) = call(
-        own0_body,
+        functools.partial(own0_body, tiles),
         [frames(wide, dtype=f32)],
         (own, outer, inner, weight_first, bias_first),
         unit * wide,

time: 39.6 us -> 35.3 us (0.89)
  starting transfers between devices: 19.5 us -> 11.9 us
  waiting for transfers between devices: 6.79 us -> 9.34 us
  Pallas kernels: 12.1 us -> 12.8 us
    ppermute x3, starting transfers between devices: 10.1 us -> 4.75 us  [the longest x1 3.1 us: block(): first = lax.ppermute(first, 'tm', ring)]
    ppermute x3, waiting for transfers between devices: 2.92 us -> 5.51 us  [the longest x1 5.14 us: block(): first = lax.ppermute(first, 'tm', ring)]
    ppermute x1, starting transfers between devices: 5.18 us -> 3.3 us  [block(): inner = lax.ppermute(inner_edge, 'tile', inner_pairs)]
    pallas_call x6 -> x7, Pallas kernels: 12.1 us -> 12.8 us  [call(): pl.pallas_call(body, out_shape=outs, in_specs=in_specs or [VMEM] * len(ar...]
  transfers between devices with their start and end apart: 7 -> 7, of which waited for: 2 -> 3; matrix products, arithmetic and copies ran while one was open for 0% -> 0% of each run, Pallas kernels for 21% -> 27%
where the time goes in v2:
time: 35.3 us; the launch traced here: 35.1 us
  Pallas kernels  12.8 us (36%)
  starting transfers between devices  11.9 us (34%)
  waiting for transfers between devices  9.34 us (26%)
  other arithmetic  0.81 us (2%)
    pallas_call x7, Pallas kernels, call(): pl.pallas_call(body, out_shape=outs, in_specs=in_specs or [VMEM] * len(ar...  12.8 us
    ppermute x1, waiting for transfers between devices, block(): first = lax.ppermute(first, 'tm', ring)  5.14 us
    ppermute x1, waiting for transfers between devices, block(): before = lax.ppermute(send, 'tm', forward)  3.83 us
    ppermute x1, starting transfers between devices, block(): inner = lax.ppermute(inner_edge, 'tile', inner_pairs)  3.3 us
    ppermute x1, starting transfers between devices, block(): before = lax.ppermute(send, 'tm', forward)  3.15 us
    ppermute x1, starting transfers between devices, block(): first = lax.ppermute(first, 'tm', ring)  3.1 us
    ppermute x1, starting transfers between devices, block(): second = lax.ppermute(second, 'tm', ring)  0.9 us
    convert_element_type x1, other arithmetic, block(): return (rest + 0.5 * before.astype(f32)).astype(jnp.bfloat16)  0.78 us
  transfers between devices with their start and end apart: 7, of which 3 were waited for; matrix products, arithmetic and copies ran while one was open for 0% of the time, Pallas kernels for 27%

profile of v2, /device:TPU:0, one launch (start us, length us, event | category | flops | bytes accessed | tf_op | source)
XLA Modules:
  0.0 35.1 jit_solution(1776345954337450548)
XLA Ops:
  0.0 1.1 %shard_map.56 = bf16[6,128,256]{2,1,0:T(8,128)(2,1)S(1)} custom-call(bf16[2,4,128,256]{3,2,1,0:T(8,128)(2,1)} %x_ref.3), custom_call_target="tpu_custom_call" | custom-call | tf_op jit(solution)/shard_map/pallas_call | solution.py:16
  1.1 0.0 copy-start
  1.1 0.0 copy-start.2
  1.1 3.1 %collective-permute-start = (bf16[6,128,256]{2,1,0:T(8,128)(2,1)S(1)}, bf16[6,128,256]{2,1,0:T(8,128)(2,1)S(1)}, u32[]{:S(2)}, u32[]{:S(2)}) collective-permute-start(bf16[6,128,256]{2,1,0:T(8,128)(2,1)S(1)} %shard_map.56), channel_id=1, source_target_pairs={{0,1},{1,2},{2,3},{3,0},{4,5},{5,6},{6,7},{7,4},{8,9},{9,10},{10,1... | collective-permute-start | bytes 1179656 | tf_op jit(solution)/shard_map/ppermute | solution.py:216
  4.2 1.3 %shard_map.55 = (bf16[2,4,128,256]{3,2,1,0:T(8,128)(2,1)S(1)}, bf16[2,128,256]{2,1,0:T(8,128)(2,1)S(1)}, bf16[2,2,128,256]{3,2,1,0:T(8,128)(2,1)S(1)}, bf16[2,2,128,256]{3,2,1,0:T(8,128)(2,1)S(1)}) custom-call(bf16[2,4,128,256]{3,2,1,0:T(8,128)(2,1)} %x_ref.3), custom_call_target="tpu_custom_call" | custom-call | flops 10000000000 | tf_op jit(solution)/shard_map/pallas_call | solution.py:16
  5.5 0.7 %collective-permute-start.4 = (bf16[2,2,128,256]{3,2,1,0:T(8,128)(2,1)S(1)}, bf16[2,2,128,256]{3,2,1,0:T(8,128)(2,1)S(1)}, u32[]{:S(2)}, u32[]{:S(2)}) collective-permute-start(bf16[2,2,128,256]{3,2,1,0:T(8,128)(2,1)S(1)} %get-tuple-element.16), channel_id=1, source_target_pairs={{4,8},{8,4},{0,12},{12,0},{5,9},{9,5},{1,13},{13,1},{6,10},{10,6},... | collective-permute-start | bytes 786440 | tf_op jit(solution)/shard_map/ppermute | solution.py:217
  6.2 0.7 %collective-permute-start.3 = (bf16[2,2,128,256]{3,2,1,0:T(8,128)(2,1)S(1)}, bf16[2,2,128,256]{3,2,1,0:T(8,128)(2,1)S(1)}, u32[]{:S(2)}, u32[]{:S(2)}) collective-permute-start(bf16[2,2,128,256]{3,2,1,0:T(8,128)(2,1)S(1)} %get-tuple-element.16), channel_id=1, source_target_pairs={{4,9},{5,10},{6,11},{8,5},{9,6},{10,7},{20,25},{21,26},{22,27},{24... | collective-permute-start | bytes 786440 | tf_op jit(solution)/shard_map/ppermute | solution.py:219
  6.9 3.3 %collective-permute-start.5 = (bf16[2,2,128,256]{3,2,1,0:T(8,128)(2,1)S(1)}, bf16[2,2,128,256]{3,2,1,0:T(8,128)(2,1)S(1)}, u32[]{:S(2)}, u32[]{:S(2)}) collective-permute-start(bf16[2,2,128,256]{3,2,1,0:T(8,128)(2,1)S(1)} %get-tuple-element.17), channel_id=1, source_target_pairs={{0,4},{8,12},{4,0},{12,8},{1,5},{9,13},{5,1},{13,9},{2,6},{10,14},... | collective-permute-start | bytes 786440 | tf_op jit(solution)/shard_map/ppermute | solution.py:218
  10.2 5.1 %collective-permute-done.first_ref = bf16[6,128,256]{2,1,0:T(8,128)(2,1)S(1)} collective-permute-done((bf16[6,128,256]{2,1,0:T(8,128)(2,1)S(1)}, bf16[6,128,256]{2,1,0:T(8,128)(2,1)S(1)}, u32[]{:S(2)}, u32[]{:S(2)}) %collective-permute-start) | collective-permute-done | bytes 393248 | tf_op jit(solution)/shard_map/ppermute | solution.py:216
  15.4 0.1 collective-permute-start.2
  15.5 0.9 %collective-permute-start.1 = (bf16[2,128,256]{2,1,0:T(8,128)(2,1)S(1)}, bf16[2,128,256]{2,1,0:T(8,128)(2,1)S(1)}, u32[]{:S(2)}, u32[]{:S(2)}) collective-permute-start(bf16[2,128,256]{2,1,0:T(8,128)(2,1)S(1)} %get-tuple-element.15), channel_id=1, source_target_pairs={{0,1},{1,2},{2,3},{3,0},{4,5},{5,6},{6,7},{7,4},{8,9},{9,10},{10,1... | collective-permute-start | bytes 393224 | tf_op jit(solution)/shard_map/ppermute | solution.py:220
  16.4 0.0 collective-permute-done.5.inner_ref
  16.4 0.0 collective-permute-done.4.outer_ref
  16.4 0.0 copy-done
  16.4 0.0 copy-done.2
  16.4 1.1 %shard_map.57.acc0_ref = f32[6,128,256]{2,1,0:T(8,128)S(1)} custom-call(bf16[2,4,128,256]{3,2,1,0:T(8,128)(2,1)S(1)} %get-tuple-element.14.x_ref, bf16[2,2,128,256]{3,2,1,0:T(8,128)(2,1)S(1)} %collective-permute-done.4.outer_ref, bf16[2,2,128,256]{3,2,1,0:T(8,128)(2,1)S(1)} %collective-permute-done.5.inner_ref, bf16[3,3,3,256,256]{4,3,2,1,0:T(8,128)(2,1)S(1)} %copy-done, ...), custom_call_target="tpu_custom_call" | custom-call | flops 905969664 | tf_op jit(solution)/shard_map/pallas_call | solution.py:16
  17.5 0.0 copy-start.1
  17.5 2.0 %shard_map.58.acc1_ref = f32[6,128,256]{2,1,0:T(8,128)S(1)} custom-call(bf16[2,4,128,256]{3,2,1,0:T(8,128)(2,1)S(1)} %get-tuple-element.14.x_ref, bf16[2,2,128,256]{3,2,1,0:T(8,128)(2,1)S(1)} %collective-permute-done.4.outer_ref, bf16[2,2,128,256]{3,2,1,0:T(8,128)(2,1)S(1)} %collective-permute-done.5.inner_ref, bf16[3,3,3,256,256]{4,3,2,1,0:T(8,128)(2,1)S(1)} %copy-done, ...), custom_call_target="tpu_custom_call" | custom-call | flops 1811939328 | tf_op jit(solution)/shard_map/pallas_call | solution.py:16
  19.5 0.0 collective-permute-done.3.outer_ref
  19.5 0.0 collective-permute-done.2.inner_ref
  19.5 0.0 copy-done.1
  19.5 3.2 %shard_map.59 = (f32[6,128,256]{2,1,0:T(8,128)S(1)}, f32[4,128,256]{2,1,0:T(8,128)S(1)}, bf16[6,128,256]{2,1,0:T(8,128)(2,1)S(1)}) custom-call(bf16[6,128,256]{2,1,0:T(8,128)(2,1)S(1)} %collective-permute-done.first_ref, bf16[2,2,128,256]{3,2,1,0:T(8,128)(2,1)S(1)} %collective-permute-done.2.inner_ref, ...), custom_call_target="tpu_custom_call" | custom-call | flops 3019898880 | tf_op jit(solution)/shard_map/pallas_call | solution.py:16
  22.8 0.4 %collective-permute-done.1.second_ref = bf16[2,128,256]{2,1,0:T(8,128)(2,1)S(1)} collective-permute-done((bf16[2,128,256]{2,1,0:T(8,128)(2,1)S(1)}, bf16[2,128,256]{2,1,0:T(8,128)(2,1)S(1)}, u32[]{:S(2)}, u32[]{:S(2)}) %collective-permute-start.1) | collective-permute-done | bytes 131104 | tf_op jit(solution)/shard_map/ppermute | solution.py:220
  23.2 0.0 copy-start.3
  23.2 2.1 %shard_map.60 = (bf16[1,4,128,256]{3,2,1,0:T(8,128)(2,1)S(1)}, bf16[6,128,256]{2,1,0:T(8,128)(2,1)S(1)}) custom-call(bf16[6,128,256]{2,1,0:T(8,128)(2,1)S(1)} %collective-permute-done.first_ref, bf16[2,128,256]{2,1,0:T(8,128)(2,1)S(1)} %collective-permute-done.1.second_ref, bf16[2,2,128,256]{3,2,1,0:T(8,128)(2,1)S(1)} %collective-permute-done.2.inner_ref, ...), custom_call_target="tpu_custom_call" | custom-call | flops 1509949440 | tf_op jit(solution)/shard_map/pallas_call | solution.py:16
  25.3 3.2 %collective-permute-start.6 = (bf16[1,4,128,256]{3,2,1,0:T(8,128)(2,1)S(1)}, bf16[1,4,128,256]{3,2,1,0:T(8,128)(2,1)S(1)}, u32[]{:S(2)}, u32[]{:S(2)}) collective-permute-start(bf16[1,4,128,256]{3,2,1,0:T(8,128)(2,1)S(1)} %get-tuple-element.22), channel_id=1, source_target_pairs={{0,1},{1,2},{2,3},{4,5},{5,6},{6,7},{8,9},{9,10},{10,11},{12,13},{... | collective-permute-start | bytes 786440 | tf_op jit(solution)/shard_map/ppermute | solution.py:256
  28.4 0.0 copy-done.3
  28.5 2.0 %shard_map.61 = f32[1,4,128,256]{3,2,1,0:T(8,128)S(1)} custom-call(bf16[2,4,128,256]{3,2,1,0:T(8,128)(2,1)S(1)} %get-tuple-element.14.x_ref, bf16[6,128,256]{2,1,0:T(8,128)(2,1)S(1)} %get-tuple-element.20.h0_ref, bf16[6,128,256]{2,1,0:T(8,128)(2,1)S(1)} %get-tuple-element.21.h1_ref, bf16[3,3,3,256,256]{4,3,2,1,0:T(8,128)(2,1)S(1)} %copy-done.1, ...), custom_call_target="tpu_custom_call" | custom-call | flops 1811939328 | tf_op jit(solution)/shard_map/pallas_call | solution.py:16
  30.5 3.8 %collective-permute-done.6 = bf16[1,4,128,256]{3,2,1,0:T(8,128)(2,1)S(1)} collective-permute-done((bf16[1,4,128,256]{3,2,1,0:T(8,128)(2,1)S(1)}, bf16[1,4,128,256]{3,2,1,0:T(8,128)(2,1)S(1)}, u32[]{:S(2)}, u32[]{:S(2)}) %collective-permute-start.6) | collective-permute-done | bytes 262176 | tf_op jit(solution)/shard_map/ppermute | solution.py:256
  34.3 0.8 %add_convert_fusion = bf16[1,4,128,256]{3,2,1,0:T(8,128)(2,1)} fusion(f32[1,4,128,256]{3,2,1,0:T(8,128)S(1)} %shard_map.61, bf16[1,4,128,256]{3,2,1,0:T(8,128)(2,1)S(1)} %collective-permute-done.6), kind=kLoop, calls=%fused_computation | loop fusion | flops 524288 | bytes 1048576 | tf_op jit(solution)/shard_map/convert_element_type | solution.py:263
  (2 shorter events, 0.0 us)
Async XLA Ops:
  1.1 15.3 %copy-start = (bf16[3,3,3,256,256]{4,3,2,1,0:T(8,128)(2,1)S(1)}, bf16[3,3,3,256,256]{4,3,2,1,0:T(8,128)(2,1)}, u32[]{:S(2)}) copy-start(bf16[3,3,3,256,256]{4,3,2,1,0:T(8,128)(2,1)} %w_ref.7) | copy-start | bytes 10616836
  1.1 15.3 %copy-start.2 = (f32[256]{0:T(256)S(1)}, f32[256]{0:T(256)}, u32[]{:S(2)}) copy-start(f32[256]{0:T(256)} %param.7) | copy-start | bytes 3076
  1.1 14.2 %collective-permute-start = (bf16[6,128,256]{2,1,0:T(8,128)(2,1)S(1)}, bf16[6,128,256]{2,1,0:T(8,128)(2,1)S(1)}, u32[]{:S(2)}, u32[]{:S(2)}) collective-permute-start(bf16[6,128,256]{2,1,0:T(8,128)(2,1)S(1)} %shard_map.56), channel_id=1, source_target_pairs={{0,1},{1,2},{2,3},{3,0},{4,5},{5,6},{6,7},{7,4},{8,9},{9,10},{10,1... | collective-permute-start | bytes 1179656 | tf_op jit(solution)/shard_map/ppermute | solution.py:216
  5.5 10.9 %collective-permute-start.4 = (bf16[2,2,128,256]{3,2,1,0:T(8,128)(2,1)S(1)}, bf16[2,2,128,256]{3,2,1,0:T(8,128)(2,1)S(1)}, u32[]{:S(2)}, u32[]{:S(2)}) collective-permute-start(bf16[2,2,128,256]{3,2,1,0:T(8,128)(2,1)S(1)} %get-tuple-element.16), channel_id=1, source_target_pairs={{4,8},{8,4},{0,12},{12,0},{5,9},{9,5},{1,13},{13,1},{6,10},{10,6},... | collective-permute-start | bytes 786440 | tf_op jit(solution)/shard_map/ppermute | solution.py:217
  6.2 13.3 %collective-permute-start.3 = (bf16[2,2,128,256]{3,2,1,0:T(8,128)(2,1)S(1)}, bf16[2,2,128,256]{3,2,1,0:T(8,128)(2,1)S(1)}, u32[]{:S(2)}, u32[]{:S(2)}) collective-permute-start(bf16[2,2,128,256]{3,2,1,0:T(8,128)(2,1)S(1)} %get-tuple-element.16), channel_id=1, source_target_pairs={{4,9},{5,10},{6,11},{8,5},{9,6},{10,7},{20,25},{21,26},{22,27},{24... | collective-permute-start | bytes 786440 | tf_op jit(solution)/shard_map/ppermute | solution.py:219
  6.9 9.5 %collective-permute-start.5 = (bf16[2,2,128,256]{3,2,1,0:T(8,128)(2,1)S(1)}, bf16[2,2,128,256]{3,2,1,0:T(8,128)(2,1)S(1)}, u32[]{:S(2)}, u32[]{:S(2)}) collective-permute-start(bf16[2,2,128,256]{3,2,1,0:T(8,128)(2,1)S(1)} %get-tuple-element.17), channel_id=1, source_target_pairs={{0,4},{8,12},{4,0},{12,8},{1,5},{9,13},{5,1},{13,9},{2,6},{10,14},... | collective-permute-start | bytes 786440 | tf_op jit(solution)/shard_map/ppermute | solution.py:218
  15.4 4.1 %collective-permute-start.2 = (bf16[2,2,128,256]{3,2,1,0:T(8,128)(2,1)S(1)}, bf16[2,2,128,256]{3,2,1,0:T(8,128)(2,1)S(1)}, u32[]{:S(2)}, u32[]{:S(2)}) collective-permute-start(bf16[2,2,128,256]{3,2,1,0:T(8,128)(2,1)S(1)} %pad_maximum_fusion), channel_id=1, source_target_pairs={{0,4},{8,12},{4,0},{12,8},{1,5},{9,13},{5,1},{13,9},{2,6},{10,14},... | collective-permute-start | bytes 786440 | tf_op jit(solution)/shard_map/ppermute | solution.py:241
  15.5 7.7 %collective-permute-start.1 = (bf16[2,128,256]{2,1,0:T(8,128)(2,1)S(1)}, bf16[2,128,256]{2,1,0:T(8,128)(2,1)S(1)}, u32[]{:S(2)}, u32[]{:S(2)}) collective-permute-start(bf16[2,128,256]{2,1,0:T(8,128)(2,1)S(1)} %get-tuple-element.15), channel_id=1, source_target_pairs={{0,1},{1,2},{2,3},{3,0},{4,5},{5,6},{6,7},{7,4},{8,9},{9,10},{10,1... | collective-permute-start | bytes 393224 | tf_op jit(solution)/shard_map/ppermute | solution.py:220
  17.5 2.0 %copy-start.1 = (bf16[3,3,3,256,256]{4,3,2,1,0:T(8,128)(2,1)S(1)}, bf16[3,3,3,256,256]{4,3,2,1,0:T(8,128)(2,1)}, u32[]{:S(2)}) copy-start(bf16[3,3,3,256,256]{4,3,2,1,0:T(8,128)(2,1)} %v_ref.5) | copy-start | bytes 10616836
  23.2 5.3 %copy-start.3 = (f32[256]{0:T(256)S(1)}, f32[256]{0:T(256)}, u32[]{:S(2)}) copy-start(f32[256]{0:T(256)} %param.9) | copy-start | bytes 3076
  25.3 9.0 %collective-permute-start.6 = (bf16[1,4,128,256]{3,2,1,0:T(8,128)(2,1)S(1)}, bf16[1,4,128,256]{3,2,1,0:T(8,128)(2,1)S(1)}, u32[]{:S(2)}, u32[]{:S(2)}) collective-permute-start(bf16[1,4,128,256]{3,2,1,0:T(8,128)(2,1)S(1)} %get-tuple-element.22), channel_id=1, source_target_pairs={{0,1},{1,2},{2,3},{4,5},{5,6},{6,7},{8,9},{9,10},{10,11},{12,13},{... | collective-permute-start | bytes 786440 | tf_op jit(solution)/shard_map/ppermute | solution.py:256

commit v3 on v2

--- a/solution.py
+++ b/solution.py
@@ -51,37 +51,45 @@
     return lax.rem(lax.axis_index("tile"), 2)
 
 
-def bounded(up, main, down, tiles):
+def either(first, second):
+    even = parity() == 0
+    return jnp.concatenate([jnp.where(even, a, b) for a, b in zip(first, second)], axis=0)
+
+
+def inner_slab(outer_half, inner_half, inner):
+    if inner.shape[0] == inner_half.shape[0] == outer_half.shape[0]:
+        return either([outer_half, inner_half, inner], [inner, inner_half, outer_half])
+    below = jnp.concatenate([outer_half, inner_half, inner], axis=0)
+    above = jnp.concatenate([inner, inner_half, outer_half], axis=0)
+    return either([below], [above])
+
+
+def outer_slab(outer, outer_half, tiles):
     tile = lax.axis_index("tile")
-    up = jnp.where(tile == 0, jnp.zeros_like(up), up)
-    down = jnp.where(tile == tiles - 1, jnp.zeros_like(down), down)
-    return jnp.concatenate([up, *main, down], axis=0)
-
-
-def slab_of(outer, outer_half, inner_half, inner, tiles):
-    even = parity() == 0
-    main = [jnp.where(even, outer_half, inner_half), jnp.where(even, inner_half, outer_half)]
-    up, down = jnp.where(even, outer, inner), jnp.where(even, inner, outer)
-    slab = bounded(up, main, down, tiles)
+    beyond = (tile == 0) | ((tile == tiles - 1) & (parity() == 1))
+    outer = jnp.where(beyond, jnp.zeros_like(outer), outer)
+    return either([outer, outer_half[:2]], [outer_half[-2:], outer])
+
+
+def received(slab):
     return jnp.where(lax.axis_index("tm") == 0, jnp.zeros_like(slab), slab)
 
 
-def own_slab(x, outer, inner, tiles):
-    even = parity() == 0
-    up, down = jnp.where(even, outer, inner), jnp.where(even, inner, outer)
-    return bounded(up, [x], down, tiles)
+def places(rows):
+    even = 1 - parity()
+    return pl.ds(2 * even, rows), pl.ds(rows * (1 - even), 2)
 
 
 def weight_rows(w_ref, a):
     return [[w_ref[a, p, q] for q in range(3)] for p in range(3)]
 
 
-def silu_rows(value, tiles):
-    tile = lax.axis_index("tile")
+def silu_rows(value, start, rows, tiles):
     hidden = (value / (1.0 + jnp.exp(-value))).astype(jnp.bfloat16)
-    row = lax.broadcasted_iota(jnp.int32, hidden.shape, 0)
-    outside = ((row == 0) & (tile == 0)) | ((row == hidden.shape[0] - 1) & (tile == tiles - 1))
-    return jnp.where(outside, jnp.zeros_like(hidden), hidden)
+    row = lax.broadcasted_iota(jnp.int32, hidden.shape, 0) + start
+    row = row + lax.axis_index("tile") * rows - 1
+    inside = (row >= 0) & (row < tiles * rows)
+    return jnp.where(inside, hidden, jnp.zeros_like(hidden))
 
 
 def move(pairs, sems):
@@ -121,36 +129,59 @@
     move(pairs, sems)
 
 
-def own1_body(tiles, x_ref, outer_ref, inner_ref, w_ref, b_ref, acc_ref):
-    rows, cols = acc_ref.shape[:2]
-    taps = []
-    for f in range(2):
-        taps += row_taps(own_slab(x_ref[f], outer_ref[f], inner_ref[f], tiles), rows)
+def own_halves(x_ref, f):
+    half = x_ref.shape[1] // 2
+    top, bottom = x_ref[f, :half], x_ref[f, half:]
+    even = parity() == 0
+    return jnp.where(even, top, bottom), jnp.where(even, bottom, top)
+
+
+def own_sums(slabs, w_ref, b_ref, acc0_ref, acc1_ref):
+    rows, cols = acc0_ref.shape[:2]
+    taps = [row_taps(slab, rows) for slab in slabs]
+    acc0_ref[...] = b_ref[...] + convolved(taps[0], weight_rows(w_ref, 2), rows, cols)
     weights = weight_rows(w_ref, 1) + weight_rows(w_ref, 2)
-    acc_ref[...] = b_ref[...] + convolved(taps, weights, rows, cols)
-
-
-def own0_body(tiles, x_ref, outer_ref, inner_ref, w_ref, b_ref, acc_ref):
-    rows, cols = acc_ref.shape[:2]
-    taps = row_taps(own_slab(x_ref[0], outer_ref[0], inner_ref[0], tiles), rows)
-    acc_ref[...] = b_ref[...] + convolved(taps, weight_rows(w_ref, 2), rows, cols)
-
-
-def late_body(
-    tiles, first_ref, inner_ref, outer_ref, w_ref, v_ref, acc0_ref, acc1_ref,
+    acc1_ref[...] = b_ref[...] + convolved(taps[0] + taps[1], weights, rows, cols)
+
+
+def own_near_body(x_ref, inner_ref, w_ref, b_ref, acc0_ref, acc1_ref):
+    slabs = [inner_slab(*own_halves(x_ref, f), inner_ref[f]) for f in range(2)]
+    own_sums(slabs, w_ref, b_ref, acc0_ref, acc1_ref)
+
+
+def own_far_body(tiles, x_ref, outer_ref, w_ref, b_ref, acc0_ref, acc1_ref):
+    slabs = [outer_slab(outer_ref[f], own_halves(x_ref, f)[0], tiles) for f in range(2)]
+    own_sums(slabs, w_ref, b_ref, acc0_ref, acc1_ref)
+
+
+def late_near_body(
+    tiles, first_ref, inner_ref, w_ref, acc0_ref, acc1_ref, sum0_ref, h1_ref
+):
+    rows, cols = acc0_ref.shape[:2]
+    half = rows // 2
+    slab = received(inner_slab(first_ref[:half], first_ref[half : 2 * half], inner_ref[0]))
+    taps = row_taps(slab, rows)
+    acc1 = acc1_ref[...] + convolved(taps, weight_rows(w_ref, 0), rows, cols)
+    h1_ref[...] = silu_rows(acc1, places(rows)[0].start, rows, tiles)
+    sum0_ref[...] = acc0_ref[...] + convolved(taps, weight_rows(w_ref, 1), rows, cols)
+
+
+def late_far_body(
+    tiles, first_ref, outer_ref, w_ref, v_ref, acc0_ref, acc1_ref, near0_ref, near1_ref,
     sum0_ref, part_ref, h1_ref,
 ):
-    rows, cols = acc0_ref.shape[:2]
-    half = (rows - 2) // 2
-    slab = slab_of(outer_ref[1], first_ref[:half], first_ref[half : 2 * half], inner_ref[0], tiles)
-    taps = row_taps(slab, rows)
-    acc1 = acc1_ref[...] + convolved(taps, weight_rows(w_ref, 0), rows, cols)
-    h1 = silu_rows(acc1, tiles)
-    h1_ref[...] = h1
-    sum0_ref[...] = acc0_ref[...] + convolved(taps, weight_rows(w_ref, 1), rows, cols)
-    taps = row_taps(h1, rows - 2)
+    rows, cols = near0_ref.shape[:2]
+    near, far = places(rows)
+    slab = received(outer_slab(outer_ref[1], first_ref[: rows // 2], tiles))
+    taps = row_taps(slab, 2)
+    acc1 = acc1_ref[...] + convolved(taps, weight_rows(w_ref, 0), 2, cols)
+    h1_ref[far] = silu_rows(acc1, far.start, rows, tiles)
+    h1_ref[near] = near1_ref[...]
+    sum0_ref[far] = acc0_ref[...] + convolved(taps, weight_rows(w_ref, 1), 2, cols)
+    sum0_ref[near] = near0_ref[...]
+    taps = row_taps(h1_ref[...], rows)
     part_ref[...] = convolved(
-        taps + taps, weight_rows(v_ref, 0) + weight_rows(v_ref, 1), rows - 2, cols
+        taps + taps, weight_rows(v_ref, 0) + weight_rows(v_ref, 1), rows, cols
     )
 
 
@@ -158,15 +189,19 @@
     tiles, first_ref, second_ref, inner_ref, outer_ref, w_ref, v_ref, sum0_ref, part_ref,
     send_ref, h0_ref,
 ):
-    rows, cols = sum0_ref.shape[:2]
-    half = (rows - 2) // 2
-    slab = slab_of(outer_ref[0], second_ref[...], first_ref[2 * half :], inner_ref[1], tiles)
-    acc0 = sum0_ref[...] + convolved(row_taps(slab, rows), weight_rows(w_ref, 0), rows, cols)
-    h0 = silu_rows(acc0, tiles)
+    rows, cols = part_ref.shape[:2]
+    half = rows // 2
+    near = inner_slab(second_ref[...], first_ref[2 * half :], inner_ref[1])
+    far = outer_slab(outer_ref[0], second_ref[...], tiles)
+    outer_rows = jnp.where(parity() == 0, far[:2], far[2:])
+    slab = either(
+        [jnp.concatenate([outer_rows, near], axis=0)], [jnp.concatenate([near, outer_rows], axis=0)]
+    )
+    taps = row_taps(received(slab), rows + 2)
+    acc0 = sum0_ref[...] + convolved(taps, weight_rows(w_ref, 0), rows + 2, cols)
+    h0 = silu_rows(acc0, 0, rows, tiles)
     h0_ref[...] = h0
-    part = part_ref[...] + convolved(
-        row_taps(h0, rows - 2), weight_rows(v_ref, 0), rows - 2, cols
-    )
+    part = part_ref[...] + convolved(row_taps(h0, rows), weight_rows(v_ref, 0), rows, cols)
     send_ref[0] = part.astype(jnp.bfloat16)
 
 
@@ -217,23 +252,23 @@
     outer = lax.ppermute(outer_edge, "tile", outer_pairs + unpaired)
     inner = lax.ppermute(inner_edge, "tile", inner_pairs)
     corner = lax.ppermute(outer_edge, ("tile", "tm"), diagonal)
-    second = lax.ppermute(second, "tm", ring)
+    second = lax.ppermute(second, "tm", forward)
 
     bias_first = bias_first.reshape(1, 1, -1)
     bias_second = bias_second.reshape(1, 1, -1)
     unit = 2 * 9 * channels * channels * cols
     wide = rows + 2
-    (acc1,) = call(
-        functools.partial(own1_body, tiles),
-        [frames(wide, dtype=f32)],
-        (own, outer, inner, weight_first, bias_first),
-        2 * unit * wide,
-    )
-    (acc0,) = call(
-        functools.partial(own0_body, tiles),
-        [frames(wide, dtype=f32)],
-        (own, outer, inner, weight_first, bias_first),
-        unit * wide,
+    near0, near1 = call(
+        own_near_body,
+        [frames(rows, dtype=f32), frames(rows, dtype=f32)],
+        (own, inner, weight_first, bias_first),
+        3 * unit * rows,
+    )
+    far0, far1 = call(
+        functools.partial(own_far_body, tiles),
+        [frames(2, dtype=f32), frames(2, dtype=f32)],
+        (own, outer, weight_first, bias_first),
+        3 * unit * 2,
     )
     even = lax.rem(lax.axis_index("tile"), 2) == 0
     late_half, early_half = first[half : 2 * half], first[2 * half :]
@@ -241,11 +276,17 @@
     inner_corner = lax.ppermute(
         jnp.where(even, halves[:, half - 2 :], halves[:, :2]), "tile", inner_pairs
     )
+    near0, near1 = call(
+        functools.partial(late_near_body, tiles),
+        [frames(rows, dtype=f32), frames(rows)],
+        (first, inner_corner, weight_first, near0, near1),
+        2 * unit * rows,
+    )
     sum0, part, h1 = call(
-        functools.partial(late_body, tiles),
+        functools.partial(late_far_body, tiles),
         [frames(wide, dtype=f32), frames(rows, dtype=f32), frames(wide)],
-        (first, inner_corner, corner, weight_first, weight_second, acc0, acc1),
-        unit * 2 * (wide + rows),
+        (first, corner, weight_first, weight_second, far0, far1, near0, near1),
+        2 * unit * (rows + 2),
     )
     send, h0 = call(
         functools.partial(early_body, tiles),

time: 35.3 us -> 37.9 us (1.074)
  the two profiles are of different devices: /device:TPU:0 before, /device:TPU:1 now
where the time goes in v3:
time: 37.9 us; the launch traced here: 37.7 us
  starting transfers between devices  14.3 us (38%)
  Pallas kernels  13.1 us (35%)
  waiting for transfers between devices  8.78 us (23%)
  other arithmetic  0.79 us (2%)
  local copies, waits for them, and re-layouts  0.55 us (1%)
    pallas_call x8, Pallas kernels, call(): pl.pallas_call(body, out_shape=outs, in_specs=in_specs or [VMEM] * len(ar...  13.1 us
    ppermute x1, waiting for transfers between devices, block(): first = lax.ppermute(first, 'tm', ring)  7.34 us
    ppermute x1, starting transfers between devices, block(): before = lax.ppermute(send, 'tm', forward)  3.22 us
    ppermute x1, starting transfers between devices, block(): second = lax.ppermute(second, 'tm', forward)  3.2 us
    ppermute x1, starting transfers between devices, block(): corner = lax.ppermute(outer_edge, ('tile', 'tm'), diagonal)  2.21 us
    ppermute x1, starting transfers between devices, block(): first = lax.ppermute(first, 'tm', ring)  2.17 us
    ppermute x1, waiting for transfers between devices, block(): before = lax.ppermute(send, 'tm', forward)  1.43 us
    ppermute x1, starting transfers between devices, block(): lax.ppermute(jnp.where(even, halves[:, half - 2:], halves[:, :2]), 'tile'...  1.32 us
  transfers between devices with their start and end apart: 7, of which 2 were waited for; matrix products, arithmetic and copies ran while one was open for 0% of the time, Pallas kernels for 26%

profile of v3, /device:TPU:1, one launch (start us, length us, event | category | flops | bytes accessed | tf_op | source)
XLA Modules:
  0.0 37.7 jit_solution(15186922105840458160)
XLA Ops:
  0.0 1.1 %shard_map.56 = bf16[6,128,256]{2,1,0:T(8,128)(2,1)S(1)} custom-call(bf16[2,4,128,256]{3,2,1,0:T(8,128)(2,1)} %x_ref.3), custom_call_target="tpu_custom_call" | custom-call | tf_op jit(solution)/shard_map/pallas_call | solution.py:16
  1.1 0.0 copy-start
  1.1 0.0 copy-start.2
  1.1 2.2 %collective-permute-start = (bf16[6,128,256]{2,1,0:T(8,128)(2,1)S(1)}, bf16[6,128,256]{2,1,0:T(8,128)(2,1)S(1)}, u32[]{:S(2)}, u32[]{:S(2)}) collective-permute-start(bf16[6,128,256]{2,1,0:T(8,128)(2,1)S(1)} %shard_map.56), channel_id=1, source_target_pairs={{0,1},{1,2},{2,3},{3,0},{4,5},{5,6},{6,7},{7,4},{8,9},{9,10},{10,1... | collective-permute-start | bytes 1179656 | tf_op jit(solution)/shard_map/ppermute | solution.py:251
  3.3 1.3 %shard_map.55 = (bf16[2,4,128,256]{3,2,1,0:T(8,128)(2,1)S(1)}, bf16[2,128,256]{2,1,0:T(8,128)(2,1)S(1)}, bf16[2,2,128,256]{3,2,1,0:T(8,128)(2,1)S(1)}, bf16[2,2,128,256]{3,2,1,0:T(8,128)(2,1)S(1)}) custom-call(bf16[2,4,128,256]{3,2,1,0:T(8,128)(2,1)} %x_ref.3), custom_call_target="tpu_custom_call" | custom-call | flops 10000000000 | tf_op jit(solution)/shard_map/pallas_call | solution.py:16
  4.5 1.0 %collective-permute-start.5 = (bf16[2,2,128,256]{3,2,1,0:T(8,128)(2,1)S(1)}, bf16[2,2,128,256]{3,2,1,0:T(8,128)(2,1)S(1)}, u32[]{:S(2)}, u32[]{:S(2)}) collective-permute-start(bf16[2,2,128,256]{3,2,1,0:T(8,128)(2,1)S(1)} %get-tuple-element.25), channel_id=1, source_target_pairs={{0,4},{8,12},{4,0},{12,8},{1,5},{9,13},{5,1},{13,9},{2,6},{10,14},... | collective-permute-start | bytes 786440 | tf_op jit(solution)/shard_map/ppermute | solution.py:253
  5.6 1.2 %collective-permute-start.4 = (bf16[2,2,128,256]{3,2,1,0:T(8,128)(2,1)S(1)}, bf16[2,2,128,256]{3,2,1,0:T(8,128)(2,1)S(1)}, u32[]{:S(2)}, u32[]{:S(2)}) collective-permute-start(bf16[2,2,128,256]{3,2,1,0:T(8,128)(2,1)S(1)} %get-tuple-element.22), channel_id=1, source_target_pairs={{4,8},{8,4},{0,12},{12,0},{5,9},{9,5},{1,13},{13,1},{6,10},{10,6},... | collective-permute-start | bytes 786440 | tf_op jit(solution)/shard_map/ppermute | solution.py:252
  6.8 7.3 %collective-permute-done.first_ref = bf16[6,128,256]{2,1,0:T(8,128)(2,1)S(1)} collective-permute-done((bf16[6,128,256]{2,1,0:T(8,128)(2,1)S(1)}, bf16[6,128,256]{2,1,0:T(8,128)(2,1)S(1)}, u32[]{:S(2)}, u32[]{:S(2)}) %collective-permute-start) | collective-permute-done | bytes 393248 | tf_op jit(solution)/shard_map/ppermute | solution.py:251
  14.2 1.3 %collective-permute-start.2 = (bf16[2,2,128,256]{3,2,1,0:T(8,128)(2,1)S(1)}, bf16[2,2,128,256]{3,2,1,0:T(8,128)(2,1)S(1)}, u32[]{:S(2)}, u32[]{:S(2)}) collective-permute-start(bf16[2,2,128,256]{3,2,1,0:T(8,128)(2,1)S(1)} %pad_maximum_fusion), channel_id=1, source_target_pairs={{0,4},{8,12},{4,0},{12,8},{1,5},{9,13},{5,1},{13,9},{2,6},{10,14},... | collective-permute-start | bytes 786440 | tf_op jit(solution)/shard_map/ppermute | solution.py:276
  15.5 2.2 %collective-permute-start.3 = (bf16[2,2,128,256]{3,2,1,0:T(8,128)(2,1)S(1)}, bf16[2,2,128,256]{3,2,1,0:T(8,128)(2,1)S(1)}, u32[]{:S(2)}, u32[]{:S(2)}) collective-permute-start(bf16[2,2,128,256]{3,2,1,0:T(8,128)(2,1)S(1)} %get-tuple-element.22), channel_id=1, source_target_pairs={{4,9},{5,10},{6,11},{8,5},{9,6},{10,7},{20,25},{21,26},{22,27},{24... | collective-permute-start | bytes 786440 | tf_op jit(solution)/shard_map/ppermute | solution.py:254
  17.7 3.2 %collective-permute-start.1 = (bf16[2,128,256]{2,1,0:T(8,128)(2,1)S(1)}, bf16[2,128,256]{2,1,0:T(8,128)(2,1)S(1)}, u32[]{:S(2)}, u32[]{:S(2)}) collective-permute-start(bf16[2,128,256]{2,1,0:T(8,128)(2,1)S(1)} %get-tuple-element.21), channel_id=1, source_target_pairs={{0,1},{1,2},{2,3},{4,5},{5,6},{6,7},{8,9},{9,10},{10,11},{12,13},{... | collective-permute-start | bytes 393224 | tf_op jit(solution)/shard_map/ppermute | solution.py:255
  20.9 0.0 collective-permute-done.4.outer_ref
  20.9 0.0 copy-done
  20.9 0.0 copy-done.2
  20.9 1.1 %shard_map.57 = (f32[2,128,256]{2,1,0:T(8,128)S(1)}, f32[2,128,256]{2,1,0:T(8,128)S(1)}) custom-call(bf16[2,4,128,256]{3,2,1,0:T(8,128)(2,1)S(1)} %get-tuple-element.20.x_ref, bf16[2,2,128,256]{3,2,1,0:T(8,128)(2,1)S(1)} %collective-permute-done.4.outer_ref, bf16[3,3,3,256,256]{4,3,2,1,0:T(8,128)(2,1)S(1)} %copy-done, f32[1,1,256]{2,1,0:T(1,128)S(1)} %bitcast.6), custom_call_target="tpu_custom_call" | custom-call | flops 905969664 | tf_op jit(solution)/shard_map/pallas_call | solution.py:16
  22.0 0.0 collective-permute-done.5.inner_ref
  22.0 2.0 %shard_map.58 = (f32[4,128,256]{2,1,0:T(8,128)S(1)}, f32[4,128,256]{2,1,0:T(8,128)S(1)}) custom-call(bf16[2,4,128,256]{3,2,1,0:T(8,128)(2,1)S(1)} %get-tuple-element.20.x_ref, bf16[2,2,128,256]{3,2,1,0:T(8,128)(2,1)S(1)} %collective-permute-done.5.inner_ref, bf16[3,3,3,256,256]{4,3,2,1,0:T(8,128)(2,1)S(1)} %copy-done, f32[1,1,256]{2,1,0:T(1,128)S(1)} %bitcast.7), custom_call_target="tpu_custom_call" | custom-call | flops 1811939328 | tf_op jit(solution)/shard_map/pallas_call | solution.py:16
  24.1 0.0 copy-start.1
  24.1 0.0 collective-permute-done.2.inner_ref
  24.1 1.5 %shard_map.59 = (f32[4,128,256]{2,1,0:T(8,128)S(1)}, bf16[4,128,256]{2,1,0:T(8,128)(2,1)S(1)}) custom-call(bf16[6,128,256]{2,1,0:T(8,128)(2,1)S(1)} %collective-permute-done.first_ref, bf16[2,2,128,256]{3,2,1,0:T(8,128)(2,1)S(1)} %collective-permute-done.2.inner_ref, bf16[3,3,3,256,256]{4,3,2,1,0:T(8,128)(2,1)S(1)} %copy-done, ...), custom_call_target="tpu_custom_call" | custom-call | flops 1207959552 | tf_op jit(solution)/shard_map/pallas_call | solution.py:16
  25.5 0.0 collective-permute-done.3.outer_ref
  25.6 0.5 %copy-done.1 = bf16[3,3,3,256,256]{4,3,2,1,0:T(8,128)(2,1)S(1)} copy-done((bf16[3,3,3,256,256]{4,3,2,1,0:T(8,128)(2,1)S(1)}, bf16[3,3,3,256,256]{4,3,2,1,0:T(8,128)(2,1)}, u32[]{:S(2)}) %copy-start.1) | copy-done | bytes 3538968
  26.1 2.0 %shard_map.60 = (f32[6,128,256]{2,1,0:T(8,128)S(1)}, f32[4,128,256]{2,1,0:T(8,128)S(1)}, bf16[6,128,256]{2,1,0:T(8,128)(2,1)S(1)}) custom-call(bf16[6,128,256]{2,1,0:T(8,128)(2,1)S(1)} %collective-permute-done.first_ref, bf16[2,2,128,256]{3,2,1,0:T(8,128)(2,1)S(1)} %collective-permute-done.3.outer_ref, bf16[3,3,3,256,256]{4,3,2,1,0:T(8,128)(2,1)S(1)} %copy-done, ...), custom_call_target="tpu_custom_call" | custom-call | flops 1811939328 | tf_op jit(solution)/shard_map/pallas_call | solution.py:16
  28.1 0.0 collective-permute-done.1.second_ref
  28.1 0.0 copy-start.3
  28.1 2.1 %shard_map.61 = (bf16[1,4,128,256]{3,2,1,0:T(8,128)(2,1)S(1)}, bf16[6,128,256]{2,1,0:T(8,128)(2,1)S(1)}) custom-call(bf16[6,128,256]{2,1,0:T(8,128)(2,1)S(1)} %collective-permute-done.first_ref, bf16[2,128,256]{2,1,0:T(8,128)(2,1)S(1)} %collective-permute-done.1.second_ref, bf16[2,2,128,256]{3,2,1,0:T(8,128)(2,1)S(1)} %collective-permute-done.2.inner_ref, ...), custom_call_target="tpu_custom_call" | custom-call | flops 1509949440 | tf_op jit(solution)/shard_map/pallas_call | solution.py:16
  30.3 3.2 %collective-permute-start.6 = (bf16[1,4,128,256]{3,2,1,0:T(8,128)(2,1)S(1)}, bf16[1,4,128,256]{3,2,1,0:T(8,128)(2,1)S(1)}, u32[]{:S(2)}, u32[]{:S(2)}) collective-permute-start(bf16[1,4,128,256]{3,2,1,0:T(8,128)(2,1)S(1)} %get-tuple-element.34), channel_id=1, source_target_pairs={{0,1},{1,2},{2,3},{4,5},{5,6},{6,7},{8,9},{9,10},{10,11},{12,13},{... | collective-permute-start | bytes 786440 | tf_op jit(solution)/shard_map/ppermute | solution.py:297
  33.5 0.0 copy-done.3
  33.5 2.0 %shard_map.62 = f32[1,4,128,256]{3,2,1,0:T(8,128)S(1)} custom-call(bf16[2,4,128,256]{3,2,1,0:T(8,128)(2,1)S(1)} %get-tuple-element.20.x_ref, bf16[6,128,256]{2,1,0:T(8,128)(2,1)S(1)} %get-tuple-element.32.h0_ref, bf16[6,128,256]{2,1,0:T(8,128)(2,1)S(1)} %get-tuple-element.33.h1_ref, bf16[3,3,3,256,256]{4,3,2,1,0:T(8,128)(2,1)S(1)} %copy-done.1, ...), custom_call_target="tpu_custom_call" | custom-call | flops 1811939328 | tf_op jit(solution)/shard_map/pallas_call | solution.py:16
  35.5 1.4 %collective-permute-done.6 = bf16[1,4,128,256]{3,2,1,0:T(8,128)(2,1)S(1)} collective-permute-done((bf16[1,4,128,256]{3,2,1,0:T(8,128)(2,1)S(1)}, bf16[1,4,128,256]{3,2,1,0:T(8,128)(2,1)S(1)}, u32[]{:S(2)}, u32[]{:S(2)}) %collective-permute-start.6) | collective-permute-done | bytes 262176 | tf_op jit(solution)/shard_map/ppermute | solution.py:297
  36.9 0.8 %add_convert_fusion = bf16[1,4,128,256]{3,2,1,0:T(8,128)(2,1)} fusion(f32[1,4,128,256]{3,2,1,0:T(8,128)S(1)} %shard_map.62, bf16[1,4,128,256]{3,2,1,0:T(8,128)(2,1)S(1)} %collective-permute-done.6), kind=kLoop, calls=%fused_computation | loop fusion | flops 524288 | bytes 1048576 | tf_op jit(solution)/shard_map/convert_element_type | solution.py:304
  (2 shorter events, 0.0 us)
Async XLA Ops:
  1.1 19.8 %copy-start = (bf16[3,3,3,256,256]{4,3,2,1,0:T(8,128)(2,1)S(1)}, bf16[3,3,3,256,256]{4,3,2,1,0:T(8,128)(2,1)}, u32[]{:S(2)}) copy-start(bf16[3,3,3,256,256]{4,3,2,1,0:T(8,128)(2,1)} %w_ref.9) | copy-start | bytes 10616836
  1.1 19.8 %copy-start.2 = (f32[256]{0:T(256)S(1)}, f32[256]{0:T(256)}, u32[]{:S(2)}) copy-start(f32[256]{0:T(256)} %param.7) | copy-start | bytes 3076
  1.1 13.0 %collective-permute-start = (bf16[6,128,256]{2,1,0:T(8,128)(2,1)S(1)}, bf16[6,128,256]{2,1,0:T(8,128)(2,1)S(1)}, u32[]{:S(2)}, u32[]{:S(2)}) collective-permute-start(bf16[6,128,256]{2,1,0:T(8,128)(2,1)S(1)} %shard_map.56), channel_id=1, source_target_pairs={{0,1},{1,2},{2,3},{3,0},{4,5},{5,6},{6,7},{7,4},{8,9},{9,10},{10,1... | collective-permute-start | bytes 1179656 | tf_op jit(solution)/shard_map/ppermute | solution.py:251
  4.5 17.5 %collective-permute-start.5 = (bf16[2,2,128,256]{3,2,1,0:T(8,128)(2,1)S(1)}, bf16[2,2,128,256]{3,2,1,0:T(8,128)(2,1)S(1)}, u32[]{:S(2)}, u32[]{:S(2)}) collective-permute-start(bf16[2,2,128,256]{3,2,1,0:T(8,128)(2,1)S(1)} %get-tuple-element.25), channel_id=1, source_target_pairs={{0,4},{8,12},{4,0},{12,8},{1,5},{9,13},{5,1},{13,9},{2,6},{10,14},... | collective-permute-start | bytes 786440 | tf_op jit(solution)/shard_map/ppermute | solution.py:253
  5.6 15.3 %collective-permute-start.4 = (bf16[2,2,128,256]{3,2,1,0:T(8,128)(2,1)S(1)}, bf16[2,2,128,256]{3,2,1,0:T(8,128)(2,1)S(1)}, u32[]{:S(2)}, u32[]{:S(2)}) collective-permute-start(bf16[2,2,128,256]{3,2,1,0:T(8,128)(2,1)S(1)} %get-tuple-element.22), channel_id=1, source_target_pairs={{4,8},{8,4},{0,12},{12,0},{5,9},{9,5},{1,13},{13,1},{6,10},{10,6},... | collective-permute-start | bytes 786440 | tf_op jit(solution)/shard_map/ppermute | solution.py:252
  14.2 9.9 %collective-permute-start.2 = (bf16[2,2,128,256]{3,2,1,0:T(8,128)(2,1)S(1)}, bf16[2,2,128,256]{3,2,1,0:T(8,128)(2,1)S(1)}, u32[]{:S(2)}, u32[]{:S(2)}) collective-permute-start(bf16[2,2,128,256]{3,2,1,0:T(8,128)(2,1)S(1)} %pad_maximum_fusion), channel_id=1, source_target_pairs={{0,4},{8,12},{4,0},{12,8},{1,5},{9,13},{5,1},{13,9},{2,6},{10,14},... | collective-permute-start | bytes 786440 | tf_op jit(solution)/shard_map/ppermute | solution.py:276
  15.5 10.1 %collective-permute-start.3 = (bf16[2,2,128,256]{3,2,1,0:T(8,128)(2,1)S(1)}, bf16[2,2,128,256]{3,2,1,0:T(8,128)(2,1)S(1)}, u32[]{:S(2)}, u32[]{:S(2)}) collective-permute-start(bf16[2,2,128,256]{3,2,1,0:T(8,128)(2,1)S(1)} %get-tuple-element.22), channel_id=1, source_target_pairs={{4,9},{5,10},{6,11},{8,5},{9,6},{10,7},{20,25},{21,26},{22,27},{24... | collective-permute-start | bytes 786440 | tf_op jit(solution)/shard_map/ppermute | solution.py:254
  17.7 10.4 %collective-permute-start.1 = (bf16[2,128,256]{2,1,0:T(8,128)(2,1)S(1)}, bf16[2,128,256]{2,1,0:T(8,128)(2,1)S(1)}, u32[]{:S(2)}, u32[]{:S(2)}) collective-permute-start(bf16[2,128,256]{2,1,0:T(8,128)(2,1)S(1)} %get-tuple-element.21), channel_id=1, source_target_pairs={{0,1},{1,2},{2,3},{4,5},{5,6},{6,7},{8,9},{9,10},{10,11},{12,13},{... | collective-permute-start | bytes 393224 | tf_op jit(solution)/shard_map/ppermute | solution.py:255
  24.1 2.0 %copy-start.1 = (bf16[3,3,3,256,256]{4,3,2,1,0:T(8,128)(2,1)S(1)}, bf16[3,3,3,256,256]{4,3,2,1,0:T(8,128)(2,1)}, u32[]{:S(2)}) copy-start(bf16[3,3,3,256,256]{4,3,2,1,0:T(8,128)(2,1)} %v_ref.5) | copy-start | bytes 10616836
  28.1 5.4 %copy-start.3 = (f32[256]{0:T(256)S(1)}, f32[256]{0:T(256)}, u32[]{:S(2)}) copy-start(f32[256]{0:T(256)} %param.9) | copy-start | bytes 3076
  30.3 6.7 %collective-permute-start.6 = (bf16[1,4,128,256]{3,2,1,0:T(8,128)(2,1)S(1)}, bf16[1,4,128,256]{3,2,1,0:T(8,128)(2,1)S(1)}, u32[]{:S(2)}, u32[]{:S(2)}) collective-permute-start(bf16[1,4,128,256]{3,2,1,0:T(8,128)(2,1)S(1)} %get-tuple-element.34), channel_id=1, source_target_pairs={{0,1},{1,2},{2,3},{4,5},{5,6},{6,7},{8,9},{9,10},{10,11},{12,13},{... | collective-permute-start | bytes 786440 | tf_op jit(solution)/shard_map/ppermute | solution.py:297

commit v4 on v3

--- a/solution.py
+++ b/solution.py
@@ -71,10 +71,6 @@
     return either([outer, outer_half[:2]], [outer_half[-2:], outer])
 
 
-def received(slab):
-    return jnp.where(lax.axis_index("tm") == 0, jnp.zeros_like(slab), slab)
-
-
 def places(rows):
     even = 1 - parity()
     return pl.ds(2 * even, rows), pl.ds(rows * (1 - even), 2)
@@ -92,41 +88,25 @@
     return jnp.where(inside, hidden, jnp.zeros_like(hidden))
 
 
-def move(pairs, sems):
-    copies = [pltpu.make_async_copy(a, b, sems.at[i]) for i, (a, b) in enumerate(pairs)]
-    for copy in copies:
-        copy.start()
-    for copy in copies:
-        copy.wait()
-
-
-def halves_of(rows):
+def cut_body(x_ref, own_ref, first_ref, sem):
+    copy = pltpu.make_async_copy(x_ref, own_ref, sem)
+    copy.start()
+    copy.wait()
+    rows = x_ref.shape[1]
     half, odd = rows // 2, parity()
-    return pl.ds(odd * half, half), pl.ds((1 - odd) * half, half)
-
-
-def cut_body(x_ref, first_ref, sems):
-    half = x_ref.shape[1] // 2
-    outer, inner = halves_of(2 * half)
-    pairs = [
-        (x_ref.at[1, outer], first_ref.at[pl.ds(0, half)]),
-        (x_ref.at[1, inner], first_ref.at[pl.ds(half, half)]),
-        (x_ref.at[0, inner], first_ref.at[pl.ds(2 * half, half)]),
-    ]
-    move(pairs, sems)
-
-
-def pick_body(x_ref, own_ref, second_ref, outer_ref, inner_ref, sems):
-    rows = x_ref.shape[1]
-    odd = parity()
-    outer, inner = pl.ds(odd * (rows - 2), 2), pl.ds((1 - odd) * (rows - 2), 2)
-    pairs = [
-        (x_ref.at[:, outer], outer_ref),
-        (x_ref.at[:, inner], inner_ref),
-        (x_ref.at[0, halves_of(rows)[0]], second_ref),
-        (x_ref, own_ref),
-    ]
-    move(pairs, sems)
+    outer_half, inner_half = pl.ds(odd * half, half), pl.ds((1 - odd) * half, half)
+    first_ref[:half] = own_ref[1, outer_half]
+    first_ref[half : 2 * half] = own_ref[1, inner_half]
+    first_ref[2 * half :] = own_ref[0, inner_half]
+
+
+def edges_body(own_ref, second_ref, outer_ref, inner_ref):
+    rows = own_ref.shape[1]
+    half, odd = rows // 2, parity()
+    second_ref[...] = own_ref[0, pl.ds(odd * half, half)]
+    for f in range(2):
+        outer_ref[f] = own_ref[f, pl.ds(odd * (rows - 2), 2)]
+        inner_ref[f] = own_ref[f, pl.ds((1 - odd) * (rows - 2), 2)]
 
 
 def own_halves(x_ref, f):
@@ -154,64 +134,92 @@
     own_sums(slabs, w_ref, b_ref, acc0_ref, acc1_ref)
 
 
+def add_earlier(pairs, taps, rows, cols):
+    started = lax.axis_index("tm") > 0
+
+    @pl.when(started)
+    def _():
+        lhs = taps()
+        for total, base, weights in pairs:
+            total[...] = base[...] + convolved(lhs, weights(), rows, cols)
+
+    @pl.when(jnp.logical_not(started))
+    def _():
+        for total, base, _ in pairs:
+            total[...] = base[...]
+
+
 def late_near_body(
-    tiles, first_ref, inner_ref, w_ref, acc0_ref, acc1_ref, sum0_ref, h1_ref
+    tiles, first_ref, inner_ref, w_ref, acc0_ref, acc1_ref, sum0_ref, h1_ref, sum1_ref
 ):
     rows, cols = acc0_ref.shape[:2]
     half = rows // 2
-    slab = received(inner_slab(first_ref[:half], first_ref[half : 2 * half], inner_ref[0]))
-    taps = row_taps(slab, rows)
-    acc1 = acc1_ref[...] + convolved(taps, weight_rows(w_ref, 0), rows, cols)
-    h1_ref[...] = silu_rows(acc1, places(rows)[0].start, rows, tiles)
-    sum0_ref[...] = acc0_ref[...] + convolved(taps, weight_rows(w_ref, 1), rows, cols)
+
+    def taps():
+        return row_taps(
+            inner_slab(first_ref[:half], first_ref[half : 2 * half], inner_ref[0]), rows
+        )
+
+    pairs = [
+        (sum1_ref, acc1_ref, lambda: weight_rows(w_ref, 0)),
+        (sum0_ref, acc0_ref, lambda: weight_rows(w_ref, 1)),
+    ]
+    add_earlier(pairs, taps, rows, cols)
+    h1_ref[...] = silu_rows(sum1_ref[...], places(rows)[0].start, rows, tiles)
 
 
 def late_far_body(
     tiles, first_ref, outer_ref, w_ref, v_ref, acc0_ref, acc1_ref, near0_ref, near1_ref,
-    sum0_ref, part_ref, h1_ref,
+    sum0_ref, part_ref, h1_ref, sum1_ref,
 ):
     rows, cols = near0_ref.shape[:2]
     near, far = places(rows)
-    slab = received(outer_slab(outer_ref[1], first_ref[: rows // 2], tiles))
-    taps = row_taps(slab, 2)
-    acc1 = acc1_ref[...] + convolved(taps, weight_rows(w_ref, 0), 2, cols)
-    h1_ref[far] = silu_rows(acc1, far.start, rows, tiles)
+
+    def taps():
+        return row_taps(outer_slab(outer_ref[1], first_ref[: rows // 2], tiles), 2)
+
+    pairs = [
+        (sum1_ref, acc1_ref, lambda: weight_rows(w_ref, 0)),
+        (sum0_ref.at[far], acc0_ref, lambda: weight_rows(w_ref, 1)),
+    ]
+    add_earlier(pairs, taps, 2, cols)
+    sum0_ref[near] = near0_ref[...]
+    h1_ref[far] = silu_rows(sum1_ref[...], far.start, rows, tiles)
     h1_ref[near] = near1_ref[...]
-    sum0_ref[far] = acc0_ref[...] + convolved(taps, weight_rows(w_ref, 1), 2, cols)
-    sum0_ref[near] = near0_ref[...]
-    taps = row_taps(h1_ref[...], rows)
-    part_ref[...] = convolved(
-        taps + taps, weight_rows(v_ref, 0) + weight_rows(v_ref, 1), rows, cols
-    )
+    part_ref[...] = convolved(row_taps(h1_ref[...], rows), weight_rows(v_ref, 1), rows, cols)
 
 
 def early_body(
-    tiles, first_ref, second_ref, inner_ref, outer_ref, w_ref, v_ref, sum0_ref, part_ref,
-    send_ref, h0_ref,
+    tiles, first_ref, second_ref, inner_ref, outer_ref, w_ref, v_ref, sum0_ref, part_ref, h1_ref,
+    send_ref, h0_ref, both_ref, total_ref,
 ):
     rows, cols = part_ref.shape[:2]
     half = rows // 2
-    near = inner_slab(second_ref[...], first_ref[2 * half :], inner_ref[1])
-    far = outer_slab(outer_ref[0], second_ref[...], tiles)
-    outer_rows = jnp.where(parity() == 0, far[:2], far[2:])
-    slab = either(
-        [jnp.concatenate([outer_rows, near], axis=0)], [jnp.concatenate([near, outer_rows], axis=0)]
-    )
-    taps = row_taps(received(slab), rows + 2)
-    acc0 = sum0_ref[...] + convolved(taps, weight_rows(w_ref, 0), rows + 2, cols)
-    h0 = silu_rows(acc0, 0, rows, tiles)
+
+    def taps():
+        near = inner_slab(second_ref[...], first_ref[2 * half :], inner_ref[1])
+        far = outer_slab(outer_ref[0], second_ref[...], tiles)
+        beyond = jnp.where(parity() == 0, far[:2], far[2:])
+        below = jnp.concatenate([beyond, near], axis=0)
+        above = jnp.concatenate([near, beyond], axis=0)
+        return row_taps(either([below], [above]), rows + 2)
+
+    pairs = [(total_ref, sum0_ref, lambda: weight_rows(w_ref, 0))]
+    add_earlier(pairs, taps, rows + 2, cols)
+    h0 = silu_rows(total_ref[...], 0, rows, tiles)
+    both = (h0.astype(jnp.float32) + h1_ref[...].astype(jnp.float32)).astype(jnp.bfloat16)
     h0_ref[...] = h0
-    part = part_ref[...] + convolved(row_taps(h0, rows), weight_rows(v_ref, 0), rows, cols)
+    both_ref[...] = both
+    part = part_ref[...] + convolved(row_taps(both, rows), weight_rows(v_ref, 0), rows, cols)
     send_ref[0] = part.astype(jnp.bfloat16)
 
 
-def rest_body(x_ref, h0_ref, h1_ref, v_ref, b_ref, out_ref):
+def rest_body(x_ref, h0_ref, both_ref, v_ref, b_ref, out_ref):
     rows, cols = x_ref.shape[1:3]
-    taps = row_taps(h0_ref[...], rows)
-    weights = weight_rows(v_ref, 1) + 2 * weight_rows(v_ref, 2)
-    part = convolved(taps + taps + row_taps(h1_ref[...], rows), weights, rows, cols)
-    both = x_ref[0].astype(jnp.float32) + x_ref[1].astype(jnp.float32)
-    out_ref[0] = (both + part) * 0.5 + b_ref[...]
+    taps = row_taps(h0_ref[...], rows) + row_taps(both_ref[...], rows)
+    part = convolved(taps, weight_rows(v_ref, 1) + weight_rows(v_ref, 2), rows, cols)
+    total = x_ref[0].astype(jnp.float32) + x_ref[1].astype(jnp.float32) + part
+    out_ref[0] = total * 0.5 + b_ref[...]
 
 
 def block(x, weight_first, bias_first, weight_second, bias_second):
@@ -225,28 +233,23 @@
     inner_pairs += [(j, i) for i, j in inner_pairs]
     outer_pairs += [(j, i) for i, j in outer_pairs]
     unpaired = [(0, tiles - 1), (tiles - 1, 0)] if tiles % 2 == 0 else []
-    diagonal = [(i * times + s, j * times + t) for i, j in outer_pairs for s, t in forward]
+    diagonal = [(i * times + s, j * times + t) for i, j in outer_pairs for s, t in ring]
+    diagonal += [(i * times + s, j * times + s) for i, j in unpaired for s in range(times)]
 
     def frames(*lead, dtype=jnp.bfloat16):
         return jax.ShapeDtypeStruct((*lead, cols, channels), dtype)
 
     f32 = jnp.float32
-    x_hbm = pltpu.with_memory_space_constraint(x, pltpu.HBM)
-    (first,) = call(
+    own, first = call(
         cut_body,
-        [frames(3 * half)],
-        (x_hbm,),
+        [frames(2, rows), frames(3 * half)],
+        (pltpu.with_memory_space_constraint(x, pltpu.HBM),),
         0,
         in_specs=[HBM],
-        scratch=[pltpu.SemaphoreType.DMA((3,))],
-    )
-    own, second, outer_edge, inner_edge = call(
-        pick_body,
-        [frames(2, rows), frames(half), frames(2, 2), frames(2, 2)],
-        (x_hbm,),
-        10**10,
-        in_specs=[HBM],
-        scratch=[pltpu.SemaphoreType.DMA((4,))],
+        scratch=[pltpu.SemaphoreType.DMA(())],
+    )
+    second, outer_edge, inner_edge = call(
+        edges_body, [frames(half), frames(2, 2), frames(2, 2)], (own,), 10**10
     )
     first = lax.ppermute(first, "tm", ring)
     outer = lax.ppermute(outer_edge, "tile", outer_pairs + unpaired)
@@ -281,25 +284,28 @@
         [frames(rows, dtype=f32), frames(rows)],
         (first, inner_corner, weight_first, near0, near1),
         2 * unit * rows,
+        scratch=[pltpu.VMEM((rows, cols, channels), f32)],
     )
     sum0, part, h1 = call(
         functools.partial(late_far_body, tiles),
         [frames(wide, dtype=f32), frames(rows, dtype=f32), frames(wide)],
         (first, corner, weight_first, weight_second, far0, far1, near0, near1),
-        2 * unit * (rows + 2),
-    )
-    send, h0 = call(
+        unit * (rows + 4),
+        scratch=[pltpu.VMEM((2, cols, channels), f32)],
+    )
+    send, h0, both = call(
         functools.partial(early_body, tiles),
-        [frames(1, rows), frames(wide)],
-        (first, second, inner_corner, corner, weight_first, weight_second, sum0, part),
+        [frames(1, rows), frames(wide), frames(wide)],
+        (first, second, inner_corner, corner, weight_first, weight_second, sum0, part, h1),
         unit * (rows + wide),
+        scratch=[pltpu.VMEM((wide, cols, channels), f32)],
     )
     before = lax.ppermute(send, "tm", forward)
     (rest,) = call(
         rest_body,
         [frames(1, rows, dtype=f32)],
-        (own, h0, h1, weight_second, bias_second),
-        3 * unit * rows,
+        (own, h0, both, weight_second, bias_second),
+        2 * unit * rows,
     )
     return (rest + 0.5 * before.astype(f32)).astype(jnp.bfloat16)
 

time: 37.9 us -> 38.5 us (1.016)
  the two profiles are of different devices: /device:TPU:1 before, /device:TPU:0 now
where the time goes in v4:
time: 38.5 us; the launch traced here: 38.3 us
  waiting for transfers between devices  16.1 us (42%)
  starting transfers between devices  13.4 us (35%)
  Pallas kernels  7.69 us (20%)
  other arithmetic  0.8 us (2%)
    ppermute x1, waiting for transfers between devices, block(): first = lax.ppermute(first, 'tm', ring)  9.39 us
    pallas_call x8, Pallas kernels, call(): pl.pallas_call(body, out_shape=outs, in_specs=in_specs or [VMEM] * len(ar...  7.69 us
    ppermute x1, starting transfers between devices, block(): before = lax.ppermute(send, 'tm', forward)  5.29 us
    ppermute x1, waiting for transfers between devices, block(): before = lax.ppermute(send, 'tm', forward)  5.09 us
    ppermute x1, starting transfers between devices, block(): first = lax.ppermute(first, 'tm', ring)  3.1 us
    ppermute x1, waiting for transfers between devices, block(): corner = lax.ppermute(outer_edge, ('tile', 'tm'), diagonal)  1.66 us
    ppermute x1, starting transfers between devices, block(): outer = lax.ppermute(outer_edge, 'tile', outer_pairs + unpaired)  1.62 us
    ppermute x1, starting transfers between devices, block(): corner = lax.ppermute(outer_edge, ('tile', 'tm'), diagonal)  1.62 us
  transfers between devices with their start and end apart: 7, of which 3 were waited for; matrix products, arithmetic and copies ran while one was open for 0% of the time, Pallas kernels for 15%

profile of v4, /device:TPU:0, one launch (start us, length us, event | category | flops | bytes accessed | tf_op | source)
XLA Modules:
  0.0 38.3 jit_solution(3803422957325253480)
XLA Ops:
  0.0 1.1 %shard_map.55 = (bf16[2,4,128,256]{3,2,1,0:T(8,128)(2,1)S(1)}, bf16[6,128,256]{2,1,0:T(8,128)(2,1)S(1)}) custom-call(bf16[2,4,128,256]{3,2,1,0:T(8,128)(2,1)} %x_ref.1), custom_call_target="tpu_custom_call" | custom-call | tf_op jit(solution)/shard_map/pallas_call | solution.py:16
  1.1 3.1 %collective-permute-start = (bf16[6,128,256]{2,1,0:T(8,128)(2,1)S(1)}, bf16[6,128,256]{2,1,0:T(8,128)(2,1)S(1)}, u32[]{:S(2)}, u32[]{:S(2)}) collective-permute-start(bf16[6,128,256]{2,1,0:T(8,128)(2,1)S(1)} %get-tuple-element.23), channel_id=1, source_target_pairs={{0,1},{1,2},{2,3},{3,0},{4,5},{5,6},{6,7},{7,4},{8,9},{9,10},{10,1... | collective-permute-start | bytes 1179656 | tf_op jit(solution)/shard_map/ppermute | solution.py:254
  4.2 0.0 copy-start
  4.2 0.0 copy-start.2
  4.2 0.1 collective-permute-start.5
  4.3 1.6 %collective-permute-start.4 = (bf16[2,2,128,256]{3,2,1,0:T(8,128)(2,1)S(1)}, bf16[2,2,128,256]{3,2,1,0:T(8,128)(2,1)S(1)}, u32[]{:S(2)}, u32[]{:S(2)}) collective-permute-start(bf16[2,2,128,256]{3,2,1,0:T(8,128)(2,1)S(1)} %get-tuple-element.25), channel_id=1, source_target_pairs={{4,8},{8,4},{0,12},{12,0},{5,9},{9,5},{1,13},{13,1},{6,10},{10,6},... | collective-permute-start | bytes 786440 | tf_op jit(solution)/shard_map/ppermute | solution.py:255
  5.9 9.4 %collective-permute-done.first_ref = bf16[6,128,256]{2,1,0:T(8,128)(2,1)S(1)} collective-permute-done((bf16[6,128,256]{2,1,0:T(8,128)(2,1)S(1)}, bf16[6,128,256]{2,1,0:T(8,128)(2,1)S(1)}, u32[]{:S(2)}, u32[]{:S(2)}) %collective-permute-start) | collective-permute-done | bytes 393248 | tf_op jit(solution)/shard_map/ppermute | solution.py:254
  15.4 0.1 collective-permute-start.2
  15.5 1.6 %collective-permute-start.3 = (bf16[2,2,128,256]{3,2,1,0:T(8,128)(2,1)S(1)}, bf16[2,2,128,256]{3,2,1,0:T(8,128)(2,1)S(1)}, u32[]{:S(2)}, u32[]{:S(2)}) collective-permute-start(bf16[2,2,128,256]{3,2,1,0:T(8,128)(2,1)S(1)} %get-tuple-element.25), channel_id=1, source_target_pairs={{4,9},{5,10},{6,11},{7,8},{8,5},{9,6},{10,7},{11,4},{0,12},{1,13},... | collective-permute-start | bytes 786440 | tf_op jit(solution)/shard_map/ppermute | solution.py:257
  17.1 1.6 %collective-permute-start.1 = (bf16[2,128,256]{2,1,0:T(8,128)(2,1)S(1)}, bf16[2,128,256]{2,1,0:T(8,128)(2,1)S(1)}, u32[]{:S(2)}, u32[]{:S(2)}) collective-permute-start(bf16[2,128,256]{2,1,0:T(8,128)(2,1)S(1)} %get-tuple-element.24), channel_id=1, source_target_pairs={{0,1},{1,2},{2,3},{4,5},{5,6},{6,7},{8,9},{9,10},{10,11},{12,13},{... | collective-permute-start | bytes 393224 | tf_op jit(solution)/shard_map/ppermute | solution.py:258
  18.7 0.0 collective-permute-done.4.outer_ref
  18.7 0.0 copy-done
  18.7 0.0 copy-done.2
  18.7 1.1 %shard_map.57 = (f32[2,128,256]{2,1,0:T(8,128)S(1)}, f32[2,128,256]{2,1,0:T(8,128)S(1)}) custom-call(bf16[2,4,128,256]{3,2,1,0:T(8,128)(2,1)S(1)} %get-tuple-element.22.own_ref.x_ref, bf16[2,2,128,256]{3,2,1,0:T(8,128)(2,1)S(1)} %collective-permute-done.4.outer_ref, bf16[3,3,3,256,256]{4,3,2,1,0:T(8,128)(2,1)S(1)} %copy-done, f32[1,1,256]{2,1,0:T(1,128)S(1)} %bitcast.6), custom_call_target="tpu_custom_call" | custom-call | flops 905969664 | tf_op jit(solution)/shard_map/pallas_call | solution.py:16
  19.8 0.0 collective-permute-done.5.inner_ref
  19.8 2.0 %shard_map.58 = (f32[4,128,256]{2,1,0:T(8,128)S(1)}, f32[4,128,256]{2,1,0:T(8,128)S(1)}) custom-call(bf16[2,4,128,256]{3,2,1,0:T(8,128)(2,1)S(1)} %get-tuple-element.22.own_ref.x_ref, bf16[2,2,128,256]{3,2,1,0:T(8,128)(2,1)S(1)} %collective-permute-done.5.inner_ref, bf16[3,3,3,256,256]{4,3,2,1,0:T(8,128)(2,1)S(1)} %copy-done, f32[1,1,256]{2,1,0:T(1,128)S(1)} %bitcast.7), custom_call_target="tpu_custom_call" | custom-call | flops 1811939328 | tf_op jit(solution)/shard_map/pallas_call | solution.py:16
  21.9 0.0 copy-start.1
  21.9 0.0 collective-permute-done.2.inner_ref
  21.9 0.2 shard_map.59
  22.1 1.7 %collective-permute-done.3.outer_ref = bf16[2,2,128,256]{3,2,1,0:T(8,128)(2,1)S(1)} collective-permute-done((bf16[2,2,128,256]{3,2,1,0:T(8,128)(2,1)S(1)}, bf16[2,2,128,256]{3,2,1,0:T(8,128)(2,1)S(1)}, u32[]{:S(2)}, u32[]{:S(2)}) %collective-permute-start.3) | collective-permute-done | bytes 262176 | tf_op jit(solution)/shard_map/ppermute | solution.py:257
  23.8 0.1 copy-done.1
  23.9 0.9 %shard_map.60 = (f32[6,128,256]{2,1,0:T(8,128)S(1)}, f32[4,128,256]{2,1,0:T(8,128)S(1)}, bf16[6,128,256]{2,1,0:T(8,128)(2,1)S(1)}) custom-call(bf16[6,128,256]{2,1,0:T(8,128)(2,1)S(1)} %collective-permute-done.first_ref, bf16[2,2,128,256]{3,2,1,0:T(8,128)(2,1)S(1)} %collective-permute-done.3.outer_ref, bf16[3,3,3,256,256]{4,3,2,1,0:T(8,128)(2,1)S(1)} %copy-done, ...), custom_call_target="tpu_custom_call" | custom-call | flops 1207959552 | tf_op jit(solution)/shard_map/pallas_call | solution.py:16
  24.8 0.0 collective-permute-done.1.second_ref
  24.8 0.0 copy-start.3
  24.8 0.9 %shard_map.61 = (bf16[1,4,128,256]{3,2,1,0:T(8,128)(2,1)S(1)}, bf16[6,128,256]{2,1,0:T(8,128)(2,1)S(1)}, bf16[6,128,256]{2,1,0:T(8,128)(2,1)S(1)}) custom-call(bf16[6,128,256]{2,1,0:T(8,128)(2,1)S(1)} %collective-permute-done.first_ref, bf16[2,128,256]{2,1,0:T(8,128)(2,1)S(1)} %collective-permute-done.1.second_ref, ...), custom_call_target="tpu_custom_call" | custom-call | flops 1509949440 | tf_op jit(solution)/shard_map/pallas_call | solution.py:16
  25.7 5.3 %collective-permute-start.6 = (bf16[1,4,128,256]{3,2,1,0:T(8,128)(2,1)S(1)}, bf16[1,4,128,256]{3,2,1,0:T(8,128)(2,1)S(1)}, u32[]{:S(2)}, u32[]{:S(2)}) collective-permute-start(bf16[1,4,128,256]{3,2,1,0:T(8,128)(2,1)S(1)} %get-tuple-element.38), channel_id=1, source_target_pairs={{0,1},{1,2},{2,3},{4,5},{5,6},{6,7},{8,9},{9,10},{10,11},{12,13},{... | collective-permute-start | bytes 786440 | tf_op jit(solution)/shard_map/ppermute | solution.py:303
  31.0 0.0 copy-done.3
  31.0 1.4 %shard_map.62 = f32[1,4,128,256]{3,2,1,0:T(8,128)S(1)} custom-call(bf16[2,4,128,256]{3,2,1,0:T(8,128)(2,1)S(1)} %get-tuple-element.22.own_ref.x_ref, bf16[6,128,256]{2,1,0:T(8,128)(2,1)S(1)} %get-tuple-element.36.h0_ref, bf16[6,128,256]{2,1,0:T(8,128)(2,1)S(1)} %get-tuple-element.37.both_ref, bf16[3,3,3,256,256]{4,3,2,1,0:T(8,128)(2,1)S(1)} %copy-done.1, ...), custom_call_target="tpu_custom_call" | custom-call | flops 1207959552 | tf_op jit(solution)/shard_map/pallas_call | solution.py:16
  32.5 5.1 %collective-permute-done.6 = bf16[1,4,128,256]{3,2,1,0:T(8,128)(2,1)S(1)} collective-permute-done((bf16[1,4,128,256]{3,2,1,0:T(8,128)(2,1)S(1)}, bf16[1,4,128,256]{3,2,1,0:T(8,128)(2,1)S(1)}, u32[]{:S(2)}, u32[]{:S(2)}) %collective-permute-start.6) | collective-permute-done | bytes 262176 | tf_op jit(solution)/shard_map/ppermute | solution.py:303
  37.5 0.8 %add_convert_fusion = bf16[1,4,128,256]{3,2,1,0:T(8,128)(2,1)} fusion(f32[1,4,128,256]{3,2,1,0:T(8,128)S(1)} %shard_map.62, bf16[1,4,128,256]{3,2,1,0:T(8,128)(2,1)S(1)} %collective-permute-done.6), kind=kLoop, calls=%fused_computation | loop fusion | flops 524288 | bytes 1048576 | tf_op jit(solution)/shard_map/convert_element_type | solution.py:310
  (3 shorter events, 0.1 us)
Async XLA Ops:
  1.1 14.2 %collective-permute-start = (bf16[6,128,256]{2,1,0:T(8,128)(2,1)S(1)}, bf16[6,128,256]{2,1,0:T(8,128)(2,1)S(1)}, u32[]{:S(2)}, u32[]{:S(2)}) collective-permute-start(bf16[6,128,256]{2,1,0:T(8,128)(2,1)S(1)} %get-tuple-element.23), channel_id=1, source_target_pairs={{0,1},{1,2},{2,3},{3,0},{4,5},{5,6},{6,7},{7,4},{8,9},{9,10},{10,1... | collective-permute-start | bytes 1179656 | tf_op jit(solution)/shard_map/ppermute | solution.py:254
  4.2 14.5 %copy-start = (bf16[3,3,3,256,256]{4,3,2,1,0:T(8,128)(2,1)S(1)}, bf16[3,3,3,256,256]{4,3,2,1,0:T(8,128)(2,1)}, u32[]{:S(2)}) copy-start(bf16[3,3,3,256,256]{4,3,2,1,0:T(8,128)(2,1)} %w_ref.9) | copy-start | bytes 10616836
  4.2 14.5 %copy-start.2 = (f32[256]{0:T(256)S(1)}, f32[256]{0:T(256)}, u32[]{:S(2)}) copy-start(f32[256]{0:T(256)} %param.7) | copy-start | bytes 3076
  4.2 15.6 %collective-permute-start.5 = (bf16[2,2,128,256]{3,2,1,0:T(8,128)(2,1)S(1)}, bf16[2,2,128,256]{3,2,1,0:T(8,128)(2,1)S(1)}, u32[]{:S(2)}, u32[]{:S(2)}) collective-permute-start(bf16[2,2,128,256]{3,2,1,0:T(8,128)(2,1)S(1)} %get-tuple-element.28), channel_id=1, source_target_pairs={{0,4},{8,12},{4,0},{12,8},{1,5},{9,13},{5,1},{13,9},{2,6},{10,14},... | collective-permute-start | bytes 786440 | tf_op jit(solution)/shard_map/ppermute | solution.py:256
  4.3 14.4 %collective-permute-start.4 = (bf16[2,2,128,256]{3,2,1,0:T(8,128)(2,1)S(1)}, bf16[2,2,128,256]{3,2,1,0:T(8,128)(2,1)S(1)}, u32[]{:S(2)}, u32[]{:S(2)}) collective-permute-start(bf16[2,2,128,256]{3,2,1,0:T(8,128)(2,1)S(1)} %get-tuple-element.25), channel_id=1, source_target_pairs={{4,8},{8,4},{0,12},{12,0},{5,9},{9,5},{1,13},{13,1},{6,10},{10,6},... | collective-permute-start | bytes 786440 | tf_op jit(solution)/shard_map/ppermute | solution.py:255
  15.4 6.5 %collective-permute-start.2 = (bf16[2,2,128,256]{3,2,1,0:T(8,128)(2,1)S(1)}, bf16[2,2,128,256]{3,2,1,0:T(8,128)(2,1)S(1)}, u32[]{:S(2)}, u32[]{:S(2)}) collective-permute-start(bf16[2,2,128,256]{3,2,1,0:T(8,128)(2,1)S(1)} %pad_maximum_fusion), channel_id=1, source_target_pairs={{0,4},{8,12},{4,0},{12,8},{1,5},{9,13},{5,1},{13,9},{2,6},{10,14},... | collective-permute-start | bytes 786440 | tf_op jit(solution)/shard_map/ppermute | solution.py:279
  15.5 8.3 %collective-permute-start.3 = (bf16[2,2,128,256]{3,2,1,0:T(8,128)(2,1)S(1)}, bf16[2,2,128,256]{3,2,1,0:T(8,128)(2,1)S(1)}, u32[]{:S(2)}, u32[]{:S(2)}) collective-permute-start(bf16[2,2,128,256]{3,2,1,0:T(8,128)(2,1)S(1)} %get-tuple-element.25), channel_id=1, source_target_pairs={{4,9},{5,10},{6,11},{7,8},{8,5},{9,6},{10,7},{11,4},{0,12},{1,13},... | collective-permute-start | bytes 786440 | tf_op jit(solution)/shard_map/ppermute | solution.py:257
  17.1 7.7 %collective-permute-start.1 = (bf16[2,128,256]{2,1,0:T(8,128)(2,1)S(1)}, bf16[2,128,256]{2,1,0:T(8,128)(2,1)S(1)}, u32[]{:S(2)}, u32[]{:S(2)}) collective-permute-start(bf16[2,128,256]{2,1,0:T(8,128)(2,1)S(1)} %get-tuple-element.24), channel_id=1, source_target_pairs={{0,1},{1,2},{2,3},{4,5},{5,6},{6,7},{8,9},{9,10},{10,11},{12,13},{... | collective-permute-start | bytes 393224 | tf_op jit(solution)/shard_map/ppermute | solution.py:258
  21.9 2.0 %copy-start.1 = (bf16[3,3,3,256,256]{4,3,2,1,0:T(8,128)(2,1)S(1)}, bf16[3,3,3,256,256]{4,3,2,1,0:T(8,128)(2,1)}, u32[]{:S(2)}) copy-start(bf16[3,3,3,256,256]{4,3,2,1,0:T(8,128)(2,1)} %v_ref.5) | copy-start | bytes 10616836
  24.8 6.3 %copy-start.3 = (f32[256]{0:T(256)S(1)}, f32[256]{0:T(256)}, u32[]{:S(2)}) copy-start(f32[256]{0:T(256)} %param.9) | copy-start | bytes 3076
  25.7 11.8 %collective-permute-start.6 = (bf16[1,4,128,256]{3,2,1,0:T(8,128)(2,1)S(1)}, bf16[1,4,128,256]{3,2,1,0:T(8,128)(2,1)S(1)}, u32[]{:S(2)}, u32[]{:S(2)}) collective-permute-start(bf16[1,4,128,256]{3,2,1,0:T(8,128)(2,1)S(1)} %get-tuple-element.38), channel_id=1, source_target_pairs={{0,1},{1,2},{2,3},{4,5},{5,6},{6,7},{8,9},{9,10},{10,11},{12,13},{... | collective-permute-start | bytes 786440 | tf_op jit(solution)/shard_map/ppermute | solution.py:303

commit v5 on v4

--- a/solution.py
+++ b/solution.py
@@ -222,6 +222,12 @@
     out_ref[0] = total * 0.5 + b_ref[...]
 
 
+def join_body(rest_ref, before_ref, out_ref):
+    before = before_ref[...].astype(jnp.float32)
+    before = jnp.where(lax.axis_index("tm") == 0, jnp.zeros_like(before), before)
+    out_ref[...] = (rest_ref[...] + 0.5 * before).astype(jnp.bfloat16)
+
+
 def block(x, weight_first, bias_first, weight_second, bias_second):
     _, rows, cols, channels = x.shape
     half = rows // 2
@@ -271,7 +277,7 @@
         functools.partial(own_far_body, tiles),
         [frames(2, dtype=f32), frames(2, dtype=f32)],
         (own, outer, weight_first, bias_first),
-        3 * unit * 2,
+        0,
     )
     even = lax.rem(lax.axis_index("tile"), 2) == 0
     late_half, early_half = first[half : 2 * half], first[2 * half :]
@@ -283,7 +289,7 @@
         functools.partial(late_near_body, tiles),
         [frames(rows, dtype=f32), frames(rows)],
         (first, inner_corner, weight_first, near0, near1),
-        2 * unit * rows,
+        0,
         scratch=[pltpu.VMEM((rows, cols, channels), f32)],
     )
     sum0, part, h1 = call(
@@ -300,14 +306,15 @@
         unit * (rows + wide),
         scratch=[pltpu.VMEM((wide, cols, channels), f32)],
     )
-    before = lax.ppermute(send, "tm", forward)
+    before = lax.ppermute(send, "tm", ring)
     (rest,) = call(
         rest_body,
         [frames(1, rows, dtype=f32)],
         (own, h0, both, weight_second, bias_second),
         2 * unit * rows,
     )
-    return (rest + 0.5 * before.astype(f32)).astype(jnp.bfloat16)
+    (pooled,) = call(join_body, [frames(1, rows)], (rest, before), 0)
+    return pooled
 
 
 def solution(mesh):

time: 38.5 us -> 37.5 us (0.974)
  starting transfers between devices: 13.4 us -> 11.5 us
  waiting for transfers between devices: 16.1 us -> 17 us
  Pallas kernels: 7.69 us -> 8.47 us
  other arithmetic: 0.8 us -> 0.03 us
    ppermute x1, starting transfers between devices: 5.29 us -> 3.42 us  [block(): before = lax.ppermute(send, 'tm', ring)]
    ppermute x1, waiting for transfers between devices: 5.09 us -> 5.9 us  [block(): before = lax.ppermute(send, 'tm', ring)]
    pallas_call x8 -> x9, Pallas kernels: 7.69 us -> 8.47 us  [call(): pl.pallas_call(body, out_shape=outs, in_specs=in_specs or [VMEM] * len(ar...]
    convert_element_type x1 -> x0, other arithmetic: 0.77 us -> none  [block(): return (rest + 0.5 * before.astype(f32)).astype(jnp.bfloat16)]
where the time goes in v5:
time: 37.5 us; the launch traced here: 37.3 us
  waiting for transfers between devices  17 us (45%)
  starting transfers between devices  11.5 us (31%)
  Pallas kernels  8.47 us (23%)
    ppermute x1, waiting for transfers between devices, block(): first = lax.ppermute(first, 'tm', ring)  9.39 us
    pallas_call x9, Pallas kernels, call(): pl.pallas_call(body, out_shape=outs, in_specs=in_specs or [VMEM] * len(ar...  8.47 us
    ppermute x1, waiting for transfers between devices, block(): before = lax.ppermute(send, 'tm', ring)  5.9 us
    ppermute x1, starting transfers between devices, block(): before = lax.ppermute(send, 'tm', ring)  3.42 us
    ppermute x1, starting transfers between devices, block(): first = lax.ppermute(first, 'tm', ring)  3.1 us
    ppermute x1, waiting for transfers between devices, block(): corner = lax.ppermute(outer_edge, ('tile', 'tm'), diagonal)  1.66 us
    ppermute x1, starting transfers between devices, block(): outer = lax.ppermute(outer_edge, 'tile', outer_pairs + unpaired)  1.62 us
    ppermute x1, starting transfers between devices, block(): corner = lax.ppermute(outer_edge, ('tile', 'tm'), diagonal)  1.62 us
  transfers between devices with their start and end apart: 7, of which 3 were waited for; matrix products, arithmetic and copies ran while one was open for 0% of the time, Pallas kernels for 15%

profile of v5, /device:TPU:0, one launch (start us, length us, event | category | flops | bytes accessed | tf_op | source)
XLA Modules:
  0.0 37.3 jit_solution(18177169298248875278)
XLA Ops:
  0.0 1.1 %shard_map.55 = (bf16[2,4,128,256]{3,2,1,0:T(8,128)(2,1)S(1)}, bf16[6,128,256]{2,1,0:T(8,128)(2,1)S(1)}) custom-call(bf16[2,4,128,256]{3,2,1,0:T(8,128)(2,1)} %x_ref.1), custom_call_target="tpu_custom_call" | custom-call | tf_op jit(solution)/shard_map/pallas_call | solution.py:16
  1.1 3.1 %collective-permute-start = (bf16[6,128,256]{2,1,0:T(8,128)(2,1)S(1)}, bf16[6,128,256]{2,1,0:T(8,128)(2,1)S(1)}, u32[]{:S(2)}, u32[]{:S(2)}) collective-permute-start(bf16[6,128,256]{2,1,0:T(8,128)(2,1)S(1)} %get-tuple-element.23), channel_id=1, source_target_pairs={{0,1},{1,2},{2,3},{3,0},{4,5},{5,6},{6,7},{7,4},{8,9},{9,10},{10,1... | collective-permute-start | bytes 1179656 | tf_op jit(solution)/shard_map/ppermute | solution.py:260
  4.2 0.0 copy-start
  4.2 0.0 copy-start.2
  4.2 0.1 collective-permute-start.5
  4.3 1.6 %collective-permute-start.4 = (bf16[2,2,128,256]{3,2,1,0:T(8,128)(2,1)S(1)}, bf16[2,2,128,256]{3,2,1,0:T(8,128)(2,1)S(1)}, u32[]{:S(2)}, u32[]{:S(2)}) collective-permute-start(bf16[2,2,128,256]{3,2,1,0:T(8,128)(2,1)S(1)} %get-tuple-element.25), channel_id=1, source_target_pairs={{4,8},{8,4},{0,12},{12,0},{5,9},{9,5},{1,13},{13,1},{6,10},{10,6},... | collective-permute-start | bytes 786440 | tf_op jit(solution)/shard_map/ppermute | solution.py:261
  5.9 9.4 %collective-permute-done.first_ref = bf16[6,128,256]{2,1,0:T(8,128)(2,1)S(1)} collective-permute-done((bf16[6,128,256]{2,1,0:T(8,128)(2,1)S(1)}, bf16[6,128,256]{2,1,0:T(8,128)(2,1)S(1)}, u32[]{:S(2)}, u32[]{:S(2)}) %collective-permute-start) | collective-permute-done | bytes 393248 | tf_op jit(solution)/shard_map/ppermute | solution.py:260
  15.4 0.1 collective-permute-start.2
  15.5 1.6 %collective-permute-start.3 = (bf16[2,2,128,256]{3,2,1,0:T(8,128)(2,1)S(1)}, bf16[2,2,128,256]{3,2,1,0:T(8,128)(2,1)S(1)}, u32[]{:S(2)}, u32[]{:S(2)}) collective-permute-start(bf16[2,2,128,256]{3,2,1,0:T(8,128)(2,1)S(1)} %get-tuple-element.25), channel_id=1, source_target_pairs={{4,9},{5,10},{6,11},{7,8},{8,5},{9,6},{10,7},{11,4},{0,12},{1,13},... | collective-permute-start | bytes 786440 | tf_op jit(solution)/shard_map/ppermute | solution.py:263
  17.1 1.6 %collective-permute-start.1 = (bf16[2,128,256]{2,1,0:T(8,128)(2,1)S(1)}, bf16[2,128,256]{2,1,0:T(8,128)(2,1)S(1)}, u32[]{:S(2)}, u32[]{:S(2)}) collective-permute-start(bf16[2,128,256]{2,1,0:T(8,128)(2,1)S(1)} %get-tuple-element.24), channel_id=1, source_target_pairs={{0,1},{1,2},{2,3},{4,5},{5,6},{6,7},{8,9},{9,10},{10,11},{12,13},{... | collective-permute-start | bytes 393224 | tf_op jit(solution)/shard_map/ppermute | solution.py:264
  18.7 0.0 collective-permute-done.5.inner_ref
  18.7 0.0 copy-done
  18.7 0.0 copy-done.2
  18.7 2.0 %shard_map.58 = (f32[4,128,256]{2,1,0:T(8,128)S(1)}, f32[4,128,256]{2,1,0:T(8,128)S(1)}) custom-call(bf16[2,4,128,256]{3,2,1,0:T(8,128)(2,1)S(1)} %get-tuple-element.22.own_ref.x_ref, bf16[2,2,128,256]{3,2,1,0:T(8,128)(2,1)S(1)} %collective-permute-done.5.inner_ref, bf16[3,3,3,256,256]{4,3,2,1,0:T(8,128)(2,1)S(1)} %copy-done, f32[1,1,256]{2,1,0:T(1,128)S(1)} %bitcast.6), custom_call_target="tpu_custom_call" | custom-call | flops 1811939328 | tf_op jit(solution)/shard_map/pallas_call | solution.py:16
  20.8 0.0 collective-permute-done.4.outer_ref
  20.8 1.1 %shard_map.57 = (f32[2,128,256]{2,1,0:T(8,128)S(1)}, f32[2,128,256]{2,1,0:T(8,128)S(1)}) custom-call(bf16[2,4,128,256]{3,2,1,0:T(8,128)(2,1)S(1)} %get-tuple-element.22.own_ref.x_ref, bf16[2,2,128,256]{3,2,1,0:T(8,128)(2,1)S(1)} %collective-permute-done.4.outer_ref, bf16[3,3,3,256,256]{4,3,2,1,0:T(8,128)(2,1)S(1)} %copy-done, f32[1,1,256]{2,1,0:T(1,128)S(1)} %bitcast.7), custom_call_target="tpu_custom_call" | custom-call | tf_op jit(solution)/shard_map/pallas_call | solution.py:16
  21.9 0.0 copy-start.1
  21.9 0.0 collective-permute-done.2.inner_ref
  21.9 0.2 shard_map.59
  22.1 1.7 %collective-permute-done.3.outer_ref = bf16[2,2,128,256]{3,2,1,0:T(8,128)(2,1)S(1)} collective-permute-done((bf16[2,2,128,256]{3,2,1,0:T(8,128)(2,1)S(1)}, bf16[2,2,128,256]{3,2,1,0:T(8,128)(2,1)S(1)}, u32[]{:S(2)}, u32[]{:S(2)}) %collective-permute-start.3) | collective-permute-done | bytes 262176 | tf_op jit(solution)/shard_map/ppermute | solution.py:263
  23.8 0.1 copy-done.1
  23.9 0.9 %shard_map.60 = (f32[6,128,256]{2,1,0:T(8,128)S(1)}, f32[4,128,256]{2,1,0:T(8,128)S(1)}, bf16[6,128,256]{2,1,0:T(8,128)(2,1)S(1)}) custom-call(bf16[6,128,256]{2,1,0:T(8,128)(2,1)S(1)} %collective-permute-done.first_ref, bf16[2,2,128,256]{3,2,1,0:T(8,128)(2,1)S(1)} %collective-permute-done.3.outer_ref, bf16[3,3,3,256,256]{4,3,2,1,0:T(8,128)(2,1)S(1)} %copy-done, ...), custom_call_target="tpu_custom_call" | custom-call | flops 1207959552 | tf_op jit(solution)/shard_map/pallas_call | solution.py:16
  24.8 0.0 collective-permute-done.1.second_ref
  24.8 0.0 copy-start.3
  24.8 0.9 %shard_map.61 = (bf16[1,4,128,256]{3,2,1,0:T(8,128)(2,1)S(1)}, bf16[6,128,256]{2,1,0:T(8,128)(2,1)S(1)}, bf16[6,128,256]{2,1,0:T(8,128)(2,1)S(1)}) custom-call(bf16[6,128,256]{2,1,0:T(8,128)(2,1)S(1)} %collective-permute-done.first_ref, bf16[2,128,256]{2,1,0:T(8,128)(2,1)S(1)} %collective-permute-done.1.second_ref, ...), custom_call_target="tpu_custom_call" | custom-call | flops 1509949440 | tf_op jit(solution)/shard_map/pallas_call | solution.py:16
  25.7 3.4 %collective-permute-start.6 = (bf16[1,4,128,256]{3,2,1,0:T(8,128)(2,1)S(1)}, bf16[1,4,128,256]{3,2,1,0:T(8,128)(2,1)S(1)}, u32[]{:S(2)}, u32[]{:S(2)}) collective-permute-start(bf16[1,4,128,256]{3,2,1,0:T(8,128)(2,1)S(1)} %get-tuple-element.38), channel_id=1, source_target_pairs={{0,1},{1,2},{2,3},{3,0},{4,5},{5,6},{6,7},{7,4},{8,9},{9,10},{10,1... | collective-permute-start | bytes 786440 | tf_op jit(solution)/shard_map/ppermute | solution.py:309
  29.2 0.0 copy-done.3
  29.2 1.4 %shard_map.62.rest_ref = f32[1,4,128,256]{3,2,1,0:T(8,128)S(1)} custom-call(bf16[2,4,128,256]{3,2,1,0:T(8,128)(2,1)S(1)} %get-tuple-element.22.own_ref.x_ref, bf16[6,128,256]{2,1,0:T(8,128)(2,1)S(1)} %get-tuple-element.36.h0_ref, bf16[6,128,256]{2,1,0:T(8,128)(2,1)S(1)} %get-tuple-element.37.both_ref, bf16[3,3,3,256,256]{4,3,2,1,0:T(8,128)(2,1)S(1)} %copy-done.1, ...), custom_call_target="tpu_custom_call" | custom-call | flops 1207959552 | tf_op jit(solution)/shard_map/pallas_call | solution.py:16
  30.6 5.9 %collective-permute-done.6.before_ref = bf16[1,4,128,256]{3,2,1,0:T(8,128)(2,1)S(1)} collective-permute-done((bf16[1,4,128,256]{3,2,1,0:T(8,128)(2,1)S(1)}, bf16[1,4,128,256]{3,2,1,0:T(8,128)(2,1)S(1)}, u32[]{:S(2)}, u32[]{:S(2)}) %collective-permute-start.6) | collective-permute-done | bytes 262176 | tf_op jit(solution)/shard_map/ppermute | solution.py:309
  36.5 0.8 %shard_map.63 = bf16[1,4,128,256]{3,2,1,0:T(8,128)(2,1)} custom-call(f32[1,4,128,256]{3,2,1,0:T(8,128)S(1)} %shard_map.62.rest_ref, bf16[1,4,128,256]{3,2,1,0:T(8,128)(2,1)S(1)} %collective-permute-done.6.before_ref), custom_call_target="tpu_custom_call" | custom-call | tf_op jit(solution)/shard_map/pallas_call | solution.py:16
  (3 shorter events, 0.1 us)
Async XLA Ops:
  1.1 14.2 %collective-permute-start = (bf16[6,128,256]{2,1,0:T(8,128)(2,1)S(1)}, bf16[6,128,256]{2,1,0:T(8,128)(2,1)S(1)}, u32[]{:S(2)}, u32[]{:S(2)}) collective-permute-start(bf16[6,128,256]{2,1,0:T(8,128)(2,1)S(1)} %get-tuple-element.23), channel_id=1, source_target_pairs={{0,1},{1,2},{2,3},{3,0},{4,5},{5,6},{6,7},{7,4},{8,9},{9,10},{10,1... | collective-permute-start | bytes 1179656 | tf_op jit(solution)/shard_map/ppermute | solution.py:260
  4.2 14.5 %copy-start = (bf16[3,3,3,256,256]{4,3,2,1,0:T(8,128)(2,1)S(1)}, bf16[3,3,3,256,256]{4,3,2,1,0:T(8,128)(2,1)}, u32[]{:S(2)}) copy-start(bf16[3,3,3,256,256]{4,3,2,1,0:T(8,128)(2,1)} %w_ref.9) | copy-start | bytes 10616836
  4.2 14.5 %copy-start.2 = (f32[256]{0:T(256)S(1)}, f32[256]{0:T(256)}, u32[]{:S(2)}) copy-start(f32[256]{0:T(256)} %param.7) | copy-start | bytes 3076
  4.2 14.5 %collective-permute-start.5 = (bf16[2,2,128,256]{3,2,1,0:T(8,128)(2,1)S(1)}, bf16[2,2,128,256]{3,2,1,0:T(8,128)(2,1)S(1)}, u32[]{:S(2)}, u32[]{:S(2)}) collective-permute-start(bf16[2,2,128,256]{3,2,1,0:T(8,128)(2,1)S(1)} %get-tuple-element.28), channel_id=1, source_target_pairs={{0,4},{8,12},{4,0},{12,8},{1,5},{9,13},{5,1},{13,9},{2,6},{10,14},... | collective-permute-start | bytes 786440 | tf_op jit(solution)/shard_map/ppermute | solution.py:262
  4.3 16.4 %collective-permute-start.4 = (bf16[2,2,128,256]{3,2,1,0:T(8,128)(2,1)S(1)}, bf16[2,2,128,256]{3,2,1,0:T(8,128)(2,1)S(1)}, u32[]{:S(2)}, u32[]{:S(2)}) collective-permute-start(bf16[2,2,128,256]{3,2,1,0:T(8,128)(2,1)S(1)} %get-tuple-element.25), channel_id=1, source_target_pairs={{4,8},{8,4},{0,12},{12,0},{5,9},{9,5},{1,13},{13,1},{6,10},{10,6},... | collective-permute-start | bytes 786440 | tf_op jit(solution)/shard_map/ppermute | solution.py:261
  15.4 6.5 %collective-permute-start.2 = (bf16[2,2,128,256]{3,2,1,0:T(8,128)(2,1)S(1)}, bf16[2,2,128,256]{3,2,1,0:T(8,128)(2,1)S(1)}, u32[]{:S(2)}, u32[]{:S(2)}) collective-permute-start(bf16[2,2,128,256]{3,2,1,0:T(8,128)(2,1)S(1)} %pad_maximum_fusion), channel_id=1, source_target_pairs={{0,4},{8,12},{4,0},{12,8},{1,5},{9,13},{5,1},{13,9},{2,6},{10,14},... | collective-permute-start | bytes 786440 | tf_op jit(solution)/shard_map/ppermute | solution.py:285
  15.5 8.3 %collective-permute-start.3 = (bf16[2,2,128,256]{3,2,1,0:T(8,128)(2,1)S(1)}, bf16[2,2,128,256]{3,2,1,0:T(8,128)(2,1)S(1)}, u32[]{:S(2)}, u32[]{:S(2)}) collective-permute-start(bf16[2,2,128,256]{3,2,1,0:T(8,128)(2,1)S(1)} %get-tuple-element.25), channel_id=1, source_target_pairs={{4,9},{5,10},{6,11},{7,8},{8,5},{9,6},{10,7},{11,4},{0,12},{1,13},... | collective-permute-start | bytes 786440 | tf_op jit(solution)/shard_map/ppermute | solution.py:263
  17.1 7.7 %collective-permute-start.1 = (bf16[2,128,256]{2,1,0:T(8,128)(2,1)S(1)}, bf16[2,128,256]{2,1,0:T(8,128)(2,1)S(1)}, u32[]{:S(2)}, u32[]{:S(2)}) collective-permute-start(bf16[2,128,256]{2,1,0:T(8,128)(2,1)S(1)} %get-tuple-element.24), channel_id=1, source_target_pairs={{0,1},{1,2},{2,3},{4,5},{5,6},{6,7},{8,9},{9,10},{10,11},{12,13},{... | collective-permute-start | bytes 393224 | tf_op jit(solution)/shard_map/ppermute | solution.py:264
  21.9 2.0 %copy-start.1 = (bf16[3,3,3,256,256]{4,3,2,1,0:T(8,128)(2,1)S(1)}, bf16[3,3,3,256,256]{4,3,2,1,0:T(8,128)(2,1)}, u32[]{:S(2)}) copy-start(bf16[3,3,3,256,256]{4,3,2,1,0:T(8,128)(2,1)} %v_ref.5) | copy-start | bytes 10616836
  24.8 4.4 %copy-start.3 = (f32[256]{0:T(256)S(1)}, f32[256]{0:T(256)}, u32[]{:S(2)}) copy-start(f32[256]{0:T(256)} %param.9) | copy-start | bytes 3076
  25.7 10.7 %collective-permute-start.6 = (bf16[1,4,128,256]{3,2,1,0:T(8,128)(2,1)S(1)}, bf16[1,4,128,256]{3,2,1,0:T(8,128)(2,1)S(1)}, u32[]{:S(2)}, u32[]{:S(2)}) collective-permute-start(bf16[1,4,128,256]{3,2,1,0:T(8,128)(2,1)S(1)} %get-tuple-element.38), channel_id=1, source_target_pairs={{0,1},{1,2},{2,3},{3,0},{4,5},{5,6},{6,7},{7,4},{8,9},{9,10},{10,1... | collective-permute-start | bytes 786440 | tf_op jit(solution)/shard_map/ppermute | solution.py:309

commit v6 on v4

v6 whole, which is shorter than its diff:
```python
import functools

import jax
import jax.numpy as jnp
from jax import lax
from jax.experimental import pallas as pl
from jax.experimental.pallas import tpu as pltpu
from jax.sharding import PartitionSpec as P


VMEM = pl.BlockSpec(memory_space=pltpu.VMEM)
HBM = pl.BlockSpec(memory_space=pltpu.HBM)


def call(body, outs, args, flops, in_specs=None, scratch=()):
    return pl.pallas_call(
        body,
        out_shape=outs,
        in_specs=in_specs or [VMEM] * len(args),
        out_specs=[VMEM] * len(outs),
        scratch_shapes=scratch,
        compiler_params=pltpu.CompilerParams(vmem_limit_bytes=16 << 20),
        cost_estimate=pl.CostEstimate(flops=flops, bytes_accessed=0, transcendentals=0),
    )(*args)


def flat(value):
    return value.reshape(-1, value.shape[-1])


def row_taps(slab, rows):
    return [flat(slab[p : p + rows]) for p in range(3)]


def convolved(lhs, weights, rows, cols):
    stacked = jnp.concatenate(lhs, axis=1)
    total = None
    for q in range(3):
        taps = jnp.concatenate([w[q] for w in weights], axis=0)
        part = jnp.dot(stacked, taps, preferred_element_type=jnp.float32)
        part = part.reshape(rows, cols, part.shape[-1])
        if q != 1:
            col = lax.broadcasted_iota(jnp.int32, part.shape, 1)
            edge = 0 if q == 0 else cols - 1
            part = jnp.where(col == edge, 0.0, pltpu.roll(part, 1 if q == 0 else cols - 1, 1))
        total = part if total is None else total + part
    return total


def parity():
    return lax.rem(lax.axis_index("tile"), 2)


def either(first, second):
    even = parity() == 0
    return jnp.concatenate([jnp.where(even, a, b) for a, b in zip(first, second)], axis=0)


def own_edge(own, side):
    odd = parity()
    last = own.shape[0] - 2
    return own[pl.ds((odd if side == 0 else 1 - odd) * last, 2)]


def outer_slab(outer, own, tiles):
    tile = lax.axis_index("tile")
    beyond = (tile == 0) | ((tile == tiles - 1) & (parity() == 1))
    outer = jnp.where(beyond, jnp.zeros_like(outer), outer)
    edge = own_edge(own, 0)
    return either([outer, edge], [edge, outer])


def inner_slab(inner, own):
    edge = own_edge(own, 1)
    return either([edge, inner], [inner, edge])


def places(rows):
    odd = parity()
    return pl.ds(2, rows - 2), pl.ds((1 - odd) * rows, 2), pl.ds(odd * rows, 2)


def weight_rows(w_ref, a):
    return [[w_ref[a, p, q] for q in range(3)] for p in range(3)]


def silu_rows(value, start, rows, tiles):
    hidden = (value / (1.0 + jnp.exp(-value))).astype(jnp.bfloat16)
    row = lax.broadcasted_iota(jnp.int32, hidden.shape, 0) + start
    row = row + lax.axis_index("tile") * rows - 1
    inside = (row >= 0) & (row < tiles * rows)
    return jnp.where(inside, hidden, jnp.zeros_like(hidden))


def edges_body(x_ref, own_ref, outer_ref, inner_ref, sem):
    copy = pltpu.make_async_copy(x_ref, own_ref, sem)
    copy.start()
    copy.wait()
    for f in range(2):
        outer_ref[f] = own_edge(own_ref.at[f], 0)
        inner_ref[f] = own_edge(own_ref.at[f], 1)


def turn_body(m_ref, inner_ref):
    for f in range(2):
        inner_ref[f] = own_edge(m_ref.at[f], 1)


def own_sums(slabs, w_ref, b_ref, acc0_ref, acc1_ref):
    rows, cols = acc0_ref.shape[:2]
    taps = [row_taps(slab, rows) for slab in slabs]
    acc0_ref[...] = b_ref[...] + convolved(taps[0], weight_rows(w_ref, 2), rows, cols)
    weights = weight_rows(w_ref, 1) + weight_rows(w_ref, 2)
    acc1_ref[...] = b_ref[...] + convolved(taps[0] + taps[1], weights, rows, cols)


def own_near_body(x_ref, inner_ref, w_ref, b_ref, acc0_ref, acc1_ref):
    even = parity() == 0
    slabs = []
    for f in range(2):
        below = jnp.concatenate([x_ref[f], inner_ref[f]], axis=0)
        above = jnp.concatenate([inner_ref[f], x_ref[f]], axis=0)
        slabs.append(jnp.where(even, below, above))
    own_sums(slabs, w_ref, b_ref, acc0_ref, acc1_ref)


def own_far_body(tiles, x_ref, outer_ref, w_ref, b_ref, acc0_ref, acc1_ref):
    slabs = [outer_slab(outer_ref[f], x_ref.at[f], tiles) for f in range(2)]
    own_sums(slabs, w_ref, b_ref, acc0_ref, acc1_ref)


def hidden(slab, bases, places_of, w_ref, tiles, whole, h0_ref, h1_ref, sum0_ref, sum1_ref):
    rows, cols = sum0_ref.shape[:2]
    started = lax.axis_index("tm") > 0

    @pl.when(started)
    def _():
        taps = [row_taps(slab(f), rows) for f in range(2)]
        weights = weight_rows(w_ref, 0) + weight_rows(w_ref, 1)
        sum0_ref[...] = bases[0]() + convolved(taps[0] + taps[1], weights, rows, cols)
        sum1_ref[...] = bases[1]() + convolved(taps[1], weight_rows(w_ref, 0), rows, cols)

    @pl.when(jnp.logical_not(started))
    def _():
        sum0_ref[...] = bases[0]()
        sum1_ref[...] = bases[1]()

    h0_ref[...] = silu_rows(sum0_ref[...], places_of.start, whole, tiles)
    h1_ref[...] = silu_rows(sum1_ref[...], places_of.start, whole, tiles)


def from_near(acc_ref, start, rows):
    return lambda: acc_ref[pl.ds(start, rows)]


def middle_body(tiles, m_ref, w_ref, _, acc0_ref, acc1_ref, h0_ref, h1_ref, sum0_ref, sum1_ref):
    rows = m_ref.shape[1]
    start = 2 * parity()
    bases = [from_near(acc_ref, start, rows - 2) for acc_ref in (acc0_ref, acc1_ref)]
    place = places(rows)[0]
    hidden(lambda f: m_ref[f], bases, place, w_ref, tiles, rows, h0_ref, h1_ref, sum0_ref, sum1_ref)


def near_body(
    tiles, m_ref, inner_ref, w_ref, acc0_ref, acc1_ref, h0_ref, h1_ref, sum0_ref, sum1_ref
):
    rows = m_ref.shape[1]
    start = (1 - parity()) * (rows - 2)
    bases = [from_near(acc_ref, start, 2) for acc_ref in (acc0_ref, acc1_ref)]
    place = places(rows)[1]

    def slab(f):
        return inner_slab(inner_ref[f], m_ref.at[f])

    hidden(slab, bases, place, w_ref, tiles, rows, h0_ref, h1_ref, sum0_ref, sum1_ref)


def far_body(
    tiles, m_ref, outer_ref, w_ref, v_ref, acc0_ref, acc1_ref, mid0_ref, mid1_ref, near0_ref,
    near1_ref, send_ref, h0_ref, both_ref, h1_ref, sum0_ref, sum1_ref,
):
    rows, cols = m_ref.shape[1:3]
    middle, near, far = places(rows)

    def slab(f):
        return outer_slab(outer_ref[f], m_ref.at[f], tiles)

    bases = [lambda: acc0_ref[...], lambda: acc1_ref[...]]
    h0_ref[middle], h0_ref[near] = mid0_ref[...], near0_ref[...]
    h1_ref[middle], h1_ref[near] = mid1_ref[...], near1_ref[...]
    hidden(
        slab, bases, far, w_ref, tiles, rows, h0_ref.at[far], h1_ref.at[far], sum0_ref, sum1_ref
    )
    h1 = h1_ref[...]
    both = (h0_ref[...].astype(jnp.float32) + h1.astype(jnp.float32)).astype(jnp.bfloat16)
    both_ref[...] = both
    taps = row_taps(both, rows) + row_taps(h1, rows)
    part = convolved(taps, weight_rows(v_ref, 0) + weight_rows(v_ref, 1), rows, cols)
    send_ref[0] = part.astype(jnp.bfloat16)


def rest_body(x_ref, h0_ref, both_ref, v_ref, b_ref, out_ref):
    rows, cols = x_ref.shape[1:3]
    taps = row_taps(h0_ref[...], rows) + row_taps(both_ref[...], rows)
    part = convolved(taps, weight_rows(v_ref, 1) + weight_rows(v_ref, 2), rows, cols)
    total = x_ref[0].astype(jnp.float32) + x_ref[1].astype(jnp.float32) + part
    out_ref[0] = total * 0.5 + b_ref[...]


def block(x, weight_first, bias_first, weight_second, bias_second):
    _, rows, cols, channels = x.shape
    tiles, times = lax.axis_size("tile"), lax.axis_size("tm")
    forward = [(i, i + 1) for i in range(times - 1)]
    ring = forward + [(times - 1, 0)]
    inner_pairs = [(i, i + 1) for i in range(0, tiles - 1, 2)]
    outer_pairs = [(i, i + 1) for i in range(1, tiles - 1, 2)]
    inner_pairs += [(j, i) for i, j in inner_pairs]
    outer_pairs += [(j, i) for i, j in outer_pairs]
    unpaired = [(0, tiles - 1), (tiles - 1, 0)] if tiles % 2 == 0 else []
    diagonal = [(i * times + s, j * times + t) for i, j in outer_pairs for s, t in ring]
    diagonal += [(i * times + s, j * times + s) for i, j in unpaired for s in range(times)]

    def frames(*lead, dtype=jnp.bfloat16):
        return jax.ShapeDtypeStruct((*lead, cols, channels), dtype)

    f32 = jnp.float32
    earlier = lax.ppermute(x, "tm", ring)
    x, outer_edge, inner_edge = call(
        edges_body,
        [frames(2, rows), frames(2, 2), frames(2, 2)],
        (pltpu.with_memory_space_constraint(x, pltpu.HBM),),
        10**10,
        in_specs=[HBM],
        scratch=[pltpu.SemaphoreType.DMA(())],
    )
    inner = lax.ppermute(inner_edge, "tile", inner_pairs)
    outer = lax.ppermute(outer_edge, "tile", outer_pairs + unpaired)
    corner = lax.ppermute(outer_edge, ("tile", "tm"), diagonal)

    bias_first = bias_first.reshape(1, 1, -1)
    bias_second = bias_second.reshape(1, 1, -1)
    unit = 2 * 9 * channels * channels * cols
    wide = rows + 2
    sums0, sums1 = call(
        own_near_body,
        [frames(rows, dtype=f32), frames(rows, dtype=f32)],
        (x, inner, weight_first, bias_first),
        3 * unit * rows,
    )
    far0, far1 = call(
        functools.partial(own_far_body, tiles),
        [frames(2, dtype=f32), frames(2, dtype=f32)],
        (x, outer, weight_first, bias_first),
        0,
    )
    (inner_edge,) = call(turn_body, [frames(2, 2)], (earlier,), 0)
    inner_corner = lax.ppermute(inner_edge, "tile", inner_pairs)

    def sums(count):
        return [pltpu.VMEM((count, cols, channels), f32)] * 2

    mid0, mid1 = call(
        functools.partial(middle_body, tiles),
        [frames(rows - 2), frames(rows - 2)],
        (earlier, weight_first, weight_second, sums0, sums1),
        0,
        scratch=sums(rows - 2),
    )
    near0, near1 = call(
        functools.partial(near_body, tiles),
        [frames(2), frames(2)],
        (earlier, inner_corner, weight_first, sums0, sums1),
        0,
        scratch=sums(2),
    )
    send, h0, both = call(
        functools.partial(far_body, tiles),
        [frames(1, rows), frames(wide), frames(wide)],
        (earlier, corner, weight_first, weight_second, far0, far1, mid0, mid1, near0, near1),
        unit * (rows + wide),
        scratch=[pltpu.VMEM((wide, cols, channels), jnp.bfloat16), *sums(2)],
    )
    before = lax.ppermute(send, "tm", forward)
    (rest,) = call(
        rest_body,
        [frames(1, rows, dtype=f32)],
        (x, h0, both, weight_second, bias_second),
        2 * unit * rows,
    )
    return (rest + 0.5 * before.astype(f32)).astype(jnp.bfloat16)


def solution(mesh):
    in_specs = (P(("clips", "tm"), "tile", None, None), P(), P(), P(), P())
    out_specs = P(("clips", "tm"), "tile", None, None)
    return jax.shard_map(block, mesh=mesh, in_specs=in_specs, out_specs=out_specs, check_vma=False)
```

time: 38.5 us -> 36.7 us (0.953)
  the two profiles are of different devices: /device:TPU:0 before, /device:TPU:25 now
where the time goes in v6:
time: 36.7 us; the launch traced here: 36 us
  waiting for transfers between devices  16.5 us (45%)
  Pallas kernels  10.9 us (30%)
  starting transfers between devices  7.68 us (21%)
  other arithmetic  0.77 us (2%)
    pallas_call x8, Pallas kernels, call(): pl.pallas_call(body, out_shape=outs, in_specs=in_specs or [VMEM] * len(ar...  10.9 us
    ppermute x1, waiting for transfers between devices, block(): earlier = lax.ppermute(x, 'tm', ring)  9.69 us
    ppermute x1, waiting for transfers between devices, block(): before = lax.ppermute(send, 'tm', forward)  6.77 us
    ppermute x1, starting transfers between devices, block(): corner = lax.ppermute(outer_edge, ('tile', 'tm'), diagonal)  2.71 us
    ppermute x1, starting transfers between devices, block(): outer = lax.ppermute(outer_edge, 'tile', outer_pairs + unpaired)  2.08 us
    ppermute x1, starting transfers between devices, block(): inner_corner = lax.ppermute(inner_edge, 'tile', inner_pairs)  1.6 us
    ppermute x1, starting transfers between devices, block(): before = lax.ppermute(send, 'tm', forward)  1.29 us
    convert_element_type x1, other arithmetic, block(): return (rest + 0.5 * before.astype(f32)).astype(jnp.bfloat16)  0.77 us
  transfers between devices with their start and end apart: 6, of which 2 were waited for; matrix products, arithmetic and copies ran while one was open for 0% of the time, Pallas kernels for 23%

profile of v6, /device:TPU:25, one launch (start us, length us, event | category | flops | bytes accessed | tf_op | source)
XLA Modules:
  0.0 36.0 jit_solution(11648281705743680215)
XLA Ops:
  0.0 0.0 copy-start.2
  0.0 0.0 copy-start
  0.0 0.0 collective-permute-start
  0.0 1.2 %shard_map.55 = (bf16[2,4,128,256]{3,2,1,0:T(8,128)(2,1)S(1)}, bf16[2,2,128,256]{3,2,1,0:T(8,128)(2,1)S(1)}, bf16[2,2,128,256]{3,2,1,0:T(8,128)(2,1)S(1)}) custom-call(bf16[2,4,128,256]{3,2,1,0:T(8,128)(2,1)} %x_ref.1), custom_call_target="tpu_custom_call" | custom-call | flops 10000000000 | tf_op jit(solution)/shard_map/pallas_call | solution.py:16
  1.3 2.1 %collective-permute-start.2 = (bf16[2,2,128,256]{3,2,1,0:T(8,128)(2,1)S(1)}, bf16[2,2,128,256]{3,2,1,0:T(8,128)(2,1)S(1)}, u32[]{:S(2)}, u32[]{:S(2)}) collective-permute-start(bf16[2,2,128,256]{3,2,1,0:T(8,128)(2,1)S(1)} %get-tuple-element.20), channel_id=1, source_target_pairs={{4,8},{8,4},{0,12},{12,0},{5,9},{9,5},{1,13},{13,1},{6,10},{10,6},... | collective-permute-start | bytes 786440 | tf_op jit(solution)/shard_map/ppermute | solution.py:237
  3.3 0.0 collective-permute-start.3
  3.3 9.7 %collective-permute-done.m_ref = bf16[2,4,128,256]{3,2,1,0:T(8,128)(2,1)S(1)} collective-permute-done((bf16[2,4,128,256]{3,2,1,0:T(8,128)(2,1)}, bf16[2,4,128,256]{3,2,1,0:T(8,128)(2,1)S(1)}, u32[]{:S(2)}, u32[]{:S(2)}) %collective-permute-start) | collective-permute-done | bytes 524320 | tf_op jit(solution)/shard_map/ppermute | solution.py:227
  13.0 1.6 %collective-permute-start.4 = (bf16[2,2,128,256]{3,2,1,0:T(8,128)(2,1)S(1)}, bf16[2,2,128,256]{3,2,1,0:T(8,128)(2,1)S(1)}, u32[]{:S(2)}, u32[]{:S(2)}) collective-permute-start(bf16[2,2,128,256]{3,2,1,0:T(8,128)(2,1)S(1)} %shard_map.59), channel_id=1, source_target_pairs={{0,4},{8,12},{4,0},{12,8},{1,5},{9,13},{5,1},{13,9},{2,6},{10,14},... | collective-permute-start | bytes 786440 | tf_op jit(solution)/shard_map/ppermute | solution.py:257
  14.6 2.7 %collective-permute-start.1 = (bf16[2,2,128,256]{3,2,1,0:T(8,128)(2,1)S(1)}, bf16[2,2,128,256]{3,2,1,0:T(8,128)(2,1)S(1)}, u32[]{:S(2)}, u32[]{:S(2)}) collective-permute-start(bf16[2,2,128,256]{3,2,1,0:T(8,128)(2,1)S(1)} %get-tuple-element.20), channel_id=1, source_target_pairs={{4,9},{5,10},{6,11},{7,8},{8,5},{9,6},{10,7},{11,4},{0,12},{1,13},... | collective-permute-start | bytes 786440 | tf_op jit(solution)/shard_map/ppermute | solution.py:238
  17.3 0.0 collective-permute-done.2.outer_ref
  17.4 0.0 copy-done.2
  17.4 0.0 copy-done
  17.4 1.1 %shard_map.56 = (f32[2,128,256]{2,1,0:T(8,128)S(1)}, f32[2,128,256]{2,1,0:T(8,128)S(1)}) custom-call(bf16[2,4,128,256]{3,2,1,0:T(8,128)(2,1)S(1)} %get-tuple-element.19.x_ref, bf16[2,2,128,256]{3,2,1,0:T(8,128)(2,1)S(1)} %collective-permute-done.2.outer_ref, bf16[3,3,3,256,256]{4,3,2,1,0:T(8,128)(2,1)S(1)} %copy-done, f32[1,1,256]{2,1,0:T(1,128)S(1)} %bitcast.2), custom_call_target="tpu_custom_call" | custom-call | tf_op jit(solution)/shard_map/pallas_call | solution.py:16
  18.5 0.0 copy-start.1
  18.5 0.0 collective-permute-done.3.inner_ref
  18.5 2.0 %shard_map.57 = (f32[4,128,256]{2,1,0:T(8,128)S(1)}, f32[4,128,256]{2,1,0:T(8,128)S(1)}) custom-call(bf16[2,4,128,256]{3,2,1,0:T(8,128)(2,1)S(1)} %get-tuple-element.19.x_ref, bf16[2,2,128,256]{3,2,1,0:T(8,128)(2,1)S(1)} %collective-permute-done.3.inner_ref, bf16[3,3,3,256,256]{4,3,2,1,0:T(8,128)(2,1)S(1)} %copy-done, f32[1,1,256]{2,1,0:T(1,128)S(1)} %bitcast.3), custom_call_target="tpu_custom_call" | custom-call | flops 1811939328 | tf_op jit(solution)/shard_map/pallas_call | solution.py:16
  20.5 0.0 copy-done.1
  20.5 1.3 %shard_map.58 = (bf16[2,128,256]{2,1,0:T(8,128)(2,1)S(1)}, bf16[2,128,256]{2,1,0:T(8,128)(2,1)S(1)}) custom-call(bf16[2,4,128,256]{3,2,1,0:T(8,128)(2,1)S(1)} %collective-permute-done.m_ref, bf16[3,3,3,256,256]{4,3,2,1,0:T(8,128)(2,1)S(1)} %copy-done, bf16[3,3,3,256,256]{4,3,2,1,0:T(8,128)(2,1)S(1)} %copy-done.1, ...), custom_call_target="tpu_custom_call" | custom-call | tf_op jit(solution)/shard_map/pallas_call | solution.py:16
  21.8 0.0 collective-permute-done.4.inner_ref
  21.8 1.3 %shard_map.60 = (bf16[2,128,256]{2,1,0:T(8,128)(2,1)S(1)}, bf16[2,128,256]{2,1,0:T(8,128)(2,1)S(1)}) custom-call(bf16[2,4,128,256]{3,2,1,0:T(8,128)(2,1)S(1)} %collective-permute-done.m_ref, bf16[2,2,128,256]{3,2,1,0:T(8,128)(2,1)S(1)} %collective-permute-done.4.inner_ref, bf16[3,3,3,256,256]{4,3,2,1,0:T(8,128)(2,1)S(1)} %copy-done, ...), custom_call_target="tpu_custom_call" | custom-call | tf_op jit(solution)/shard_map/pallas_call | solution.py:16
  23.1 0.0 collective-permute-done.1.outer_ref
  23.1 0.0 copy-start.3
  23.1 2.6 %shard_map.61 = (bf16[1,4,128,256]{3,2,1,0:T(8,128)(2,1)S(1)}, bf16[6,128,256]{2,1,0:T(8,128)(2,1)S(1)}, bf16[6,128,256]{2,1,0:T(8,128)(2,1)S(1)}) custom-call(bf16[2,4,128,256]{3,2,1,0:T(8,128)(2,1)S(1)} %collective-permute-done.m_ref, bf16[2,2,128,256]{3,2,1,0:T(8,128)(2,1)S(1)} %collective-permute-done.1.outer_ref, ...), custom_call_target="tpu_custom_call" | custom-call | flops 1509949440 | tf_op jit(solution)/shard_map/pallas_call | solution.py:16
  25.7 1.3 %collective-permute-start.5 = (bf16[1,4,128,256]{3,2,1,0:T(8,128)(2,1)S(1)}, bf16[1,4,128,256]{3,2,1,0:T(8,128)(2,1)S(1)}, u32[]{:S(2)}, u32[]{:S(2)}) collective-permute-start(bf16[1,4,128,256]{3,2,1,0:T(8,128)(2,1)S(1)} %get-tuple-element.32), channel_id=1, source_target_pairs={{0,1},{1,2},{2,3},{4,5},{5,6},{6,7},{8,9},{9,10},{10,11},{12,13},{... | collective-permute-start | bytes 786440 | tf_op jit(solution)/shard_map/ppermute | solution.py:283
  27.0 0.0 copy-done.3
  27.0 1.4 %shard_map.62 = f32[1,4,128,256]{3,2,1,0:T(8,128)S(1)} custom-call(bf16[2,4,128,256]{3,2,1,0:T(8,128)(2,1)S(1)} %get-tuple-element.19.x_ref, bf16[6,128,256]{2,1,0:T(8,128)(2,1)S(1)} %get-tuple-element.30.h0_ref, bf16[6,128,256]{2,1,0:T(8,128)(2,1)S(1)} %get-tuple-element.31.both_ref, bf16[3,3,3,256,256]{4,3,2,1,0:T(8,128)(2,1)S(1)} %copy-done.1, ...), custom_call_target="tpu_custom_call" | custom-call | flops 1207959552 | tf_op jit(solution)/shard_map/pallas_call | solution.py:16
  28.4 6.8 %collective-permute-done.5 = bf16[1,4,128,256]{3,2,1,0:T(8,128)(2,1)S(1)} collective-permute-done((bf16[1,4,128,256]{3,2,1,0:T(8,128)(2,1)S(1)}, bf16[1,4,128,256]{3,2,1,0:T(8,128)(2,1)S(1)}, u32[]{:S(2)}, u32[]{:S(2)}) %collective-permute-start.5) | collective-permute-done | bytes 262176 | tf_op jit(solution)/shard_map/ppermute | solution.py:283
  35.2 0.8 %add_convert_fusion = bf16[1,4,128,256]{3,2,1,0:T(8,128)(2,1)} fusion(f32[1,4,128,256]{3,2,1,0:T(8,128)S(1)} %shard_map.62, bf16[1,4,128,256]{3,2,1,0:T(8,128)(2,1)S(1)} %collective-permute-done.5), kind=kLoop, calls=%fused_computation | loop fusion | flops 524288 | bytes 1048576 | tf_op jit(solution)/shard_map/convert_element_type | solution.py:290
  (1 shorter events, 0.0 us)
Async XLA Ops:
  0.0 17.4 %copy-start.2 = (f32[256]{0:T(256)S(1)}, f32[256]{0:T(256)}, u32[]{:S(2)}) copy-start(f32[256]{0:T(256)} %param.7) | copy-start | bytes 3076
  0.0 17.4 %copy-start = (bf16[3,3,3,256,256]{4,3,2,1,0:T(8,128)(2,1)S(1)}, bf16[3,3,3,256,256]{4,3,2,1,0:T(8,128)(2,1)}, u32[]{:S(2)}) copy-start(bf16[3,3,3,256,256]{4,3,2,1,0:T(8,128)(2,1)} %w_ref.9) | copy-start | bytes 10616836
  0.0 13.0 %collective-permute-start = (bf16[2,4,128,256]{3,2,1,0:T(8,128)(2,1)}, bf16[2,4,128,256]{3,2,1,0:T(8,128)(2,1)S(1)}, u32[]{:S(2)}, u32[]{:S(2)}) collective-permute-start(bf16[2,4,128,256]{3,2,1,0:T(8,128)(2,1)} %x_ref.1), channel_id=1, source_target_pairs={{0,1},{1,2},{2,3},{3,0},{4,5},{5,6},{6,7},{7,4},{8,9},{9,10},{10,1... | collective-permute-start | bytes 1572872 | tf_op jit(solution)/shard_map/ppermute | solution.py:227
  1.3 16.1 %collective-permute-start.2 = (bf16[2,2,128,256]{3,2,1,0:T(8,128)(2,1)S(1)}, bf16[2,2,128,256]{3,2,1,0:T(8,128)(2,1)S(1)}, u32[]{:S(2)}, u32[]{:S(2)}) collective-permute-start(bf16[2,2,128,256]{3,2,1,0:T(8,128)(2,1)S(1)} %get-tuple-element.20), channel_id=1, source_target_pairs={{4,8},{8,4},{0,12},{12,0},{5,9},{9,5},{1,13},{13,1},{6,10},{10,6},... | collective-permute-start | bytes 786440 | tf_op jit(solution)/shard_map/ppermute | solution.py:237
  3.3 15.1 %collective-permute-start.3 = (bf16[2,2,128,256]{3,2,1,0:T(8,128)(2,1)S(1)}, bf16[2,2,128,256]{3,2,1,0:T(8,128)(2,1)S(1)}, u32[]{:S(2)}, u32[]{:S(2)}) collective-permute-start(bf16[2,2,128,256]{3,2,1,0:T(8,128)(2,1)S(1)} %get-tuple-element.23), channel_id=1, source_target_pairs={{0,4},{8,12},{4,0},{12,8},{1,5},{9,13},{5,1},{13,9},{2,6},{10,14},... | collective-permute-start | bytes 786440 | tf_op jit(solution)/shard_map/ppermute | solution.py:236
  13.0 8.7 %collective-permute-start.4 = (bf16[2,2,128,256]{3,2,1,0:T(8,128)(2,1)S(1)}, bf16[2,2,128,256]{3,2,1,0:T(8,128)(2,1)S(1)}, u32[]{:S(2)}, u32[]{:S(2)}) collective-permute-start(bf16[2,2,128,256]{3,2,1,0:T(8,128)(2,1)S(1)} %shard_map.59), channel_id=1, source_target_pairs={{0,4},{8,12},{4,0},{12,8},{1,5},{9,13},{5,1},{13,9},{2,6},{10,14},... | collective-permute-start | bytes 786440 | tf_op jit(solution)/shard_map/ppermute | solution.py:257
  14.6 8.4 %collective-permute-start.1 = (bf16[2,2,128,256]{3,2,1,0:T(8,128)(2,1)S(1)}, bf16[2,2,128,256]{3,2,1,0:T(8,128)(2,1)S(1)}, u32[]{:S(2)}, u32[]{:S(2)}) collective-permute-start(bf16[2,2,128,256]{3,2,1,0:T(8,128)(2,1)S(1)} %get-tuple-element.20), channel_id=1, source_target_pairs={{4,9},{5,10},{6,11},{7,8},{8,5},{9,6},{10,7},{11,4},{0,12},{1,13},... | collective-permute-start | bytes 786440 | tf_op jit(solution)/shard_map/ppermute | solution.py:238
  18.5 2.0 %copy-start.1 = (bf16[3,3,3,256,256]{4,3,2,1,0:T(8,128)(2,1)S(1)}, bf16[3,3,3,256,256]{4,3,2,1,0:T(8,128)(2,1)}, u32[]{:S(2)}) copy-start(bf16[3,3,3,256,256]{4,3,2,1,0:T(8,128)(2,1)} %v_ref.3) | copy-start | bytes 10616836
  23.1 4.0 %copy-start.3 = (f32[256]{0:T(256)S(1)}, f32[256]{0:T(256)}, u32[]{:S(2)}) copy-start(f32[256]{0:T(256)} %param.9) | copy-start | bytes 3076
  25.7 9.5 %collective-permute-start.5 = (bf16[1,4,128,256]{3,2,1,0:T(8,128)(2,1)S(1)}, bf16[1,4,128,256]{3,2,1,0:T(8,128)(2,1)S(1)}, u32[]{:S(2)}, u32[]{:S(2)}) collective-permute-start(bf16[1,4,128,256]{3,2,1,0:T(8,128)(2,1)S(1)} %get-tuple-element.32), channel_id=1, source_target_pairs={{0,1},{1,2},{2,3},{4,5},{5,6},{6,7},{8,9},{9,10},{10,11},{12,13},{... | collective-permute-start | bytes 786440 | tf_op jit(solution)/shard_map/ppermute | solution.py:283
